TPU v7x, 32 devices: a whole 2x2x4 slice. The times are simulated.
32 devices in a mesh: grid: 1, orb: 32 (over z, y, x, core).
Axes of the slice: x: 2, y: 2, z: 4, core: 2. Of those that a mesh axis runs over, the one named last changes fastest.
Arguments:
- orbitals: bfloat16 [512, 64, 4096], P('orb', 'grid'), may hold values from -6 to 6
- pairs: int32 [128, 4], P('orb'), may hold values from -16 to 511, as said below
- tiles: int32 [32, 2], replicated, may hold values from 0 to 31, as said below
Outputs:
- exch_force: float32 [512, 64, 4096], P('orb', 'grid')
- intersection_tiles: float32 [32, 256], P(('grid', 'orb'))
- self_intersection: float32 [512], P('orb')
Inputs may be any that keep to these rules, and one draw needn't show every extreme that they name: In the pairs of one device (aligned blocks of 4 rows) at most 2 of the orbital entries (columns i and j) belong to one owner (an owner holds 16 consecutive orbitals), and those entries name at most 2 distinct orbitals of that owner, so an orbital may recur; both bounds are reached in every block. Offsets lie in -16 to 16. `tiles`: A listed tile's column block differs from its row block.
All inputs are finite; a program needn't handle non-finite values.
Results may differ from a plain program's by a relative error of at most 0.0058.
Values may be sent and summed in bfloat16 or wider, within the bound.
A program may use at most 256 MiB of HBM per device.

v0:
```python
import jax
import jax.numpy as jnp
from jax import lax
from jax.sharding import PartitionSpec as P

BOX = 64
SWEEPS = 3


SCREENING = 0.02
MIXING = 0.25


def padded_2(array, sides, width):
    for axis, dim in sides:
        devices, length = (lax.axis_size(axis), array.shape[dim])
        up = [(i, (i + 1) % devices) for i in range(devices - 1)]
        down = [(j, i) for i, j in up]
        last = lax.slice_in_dim(array, length - width, length, axis=dim)
        first = lax.slice_in_dim(array, 0, width, axis=dim)
        before = lax.ppermute(last, axis, up)
        after = lax.ppermute(first, axis, down)
        array = jnp.concatenate([before, array, after], axis=dim)
    return array


def operate_slab(field_in):
    padded = padded_2(field_in, (("grid", 1),), 1)
    beside = padded[:, 2:, :] + padded[:, :-2, :]
    zero_rows = jnp.zeros(field_in.shape[:-1] + (BOX,), jnp.float32)
    beside = beside + jnp.concatenate([field_in[..., BOX:], zero_rows], axis=-1)
    beside = beside + jnp.concatenate([zero_rows, field_in[..., :-BOX]], axis=-1)
    column = jnp.arange(BOX * BOX, dtype=jnp.int32) % BOX
    zero_cells = jnp.zeros(field_in.shape[:-1] + (1,), jnp.float32)
    upward = jnp.concatenate([field_in[..., 1:], zero_cells], axis=-1)
    downward = jnp.concatenate([zero_cells, field_in[..., :-1]], axis=-1)
    beside = (
        beside + jnp.where(column < BOX - 1, upward, 0.0) + jnp.where(column > 0, downward, 0.0)
    )
    return (6.0 + SCREENING) * field_in - beside


def chebyshev(density):
    center = 6.0 + SCREENING
    radius = 6.0
    ratio = center / radius
    residual = density
    direction = density / center
    solution = direction
    previous = 1.0 / ratio
    for sweep_index in range(SWEEPS):
        residual = residual - operate_slab(direction)
        current = 1.0 / (2.0 * ratio - previous)
        direction = current * previous * direction + 2.0 * current / radius * residual
        solution = solution + direction
        previous = current
    return solution


def move(field_in, offset_y, offset_z):
    cells = jnp.arange(BOX * BOX, dtype=jnp.int32)
    row_index = cells // BOX + offset_y
    col_index = cells % BOX + offset_z
    valid = (row_index >= 0) & (row_index < BOX) & (col_index >= 0) & (col_index < BOX)
    rolled = jnp.roll(field_in, -(offset_y * BOX + offset_z), axis=-1)
    return jnp.where(valid, rolled, 0.0)


def body(orbitals, pairs, tiles):
    n_orb = lax.axis_size("orb")
    orb_dev, planes, flat_cells = orbitals.shape
    pair_count = pairs.shape[0]
    ref_count = 2 * pair_count
    ref_orb = pairs[:, :2].reshape(ref_count)
    owner_index = ref_orb // orb_dev
    local_index = ref_orb % orb_dev
    capacity = (2 * pair_count + n_orb - 1) // n_orb + 1
    same_owner = owner_index[:, None] == owner_index[None, :]
    earlier = jnp.arange(ref_count)[None, :] < jnp.arange(ref_count)[:, None]
    slot_index = jnp.sum(same_owner & earlier, axis=1)
    target = owner_index * capacity + slot_index
    positions = jnp.arange(n_orb * capacity, dtype=jnp.int32)
    placed = target[None, :] == positions[:, None]
    request = jnp.max(jnp.where(placed, local_index[None, :], 0), axis=1).reshape(n_orb, capacity)
    asked = lax.all_to_all(request, "orb", split_axis=0, concat_axis=0, tiled=True)
    outgoing = jnp.take(orbitals, asked.reshape(-1), axis=0).reshape(
        n_orb, capacity, planes, flat_cells
    )
    incoming = lax.all_to_all(outgoing, "orb", split_axis=0, concat_axis=0, tiled=True)
    fetched = jnp.take(incoming.reshape(n_orb * capacity, planes, flat_cells), target, axis=0)
    fetched = fetched.reshape(pair_count, 2, planes, flat_cells)
    first_box = fetched[:, 0].astype(jnp.float32)
    second_box = fetched[:, 1].astype(jnp.float32)
    offset_y = pairs[:, 2]
    offset_z = pairs[:, 3]
    shifted = jax.vmap(move)(second_box, offset_y, offset_z)
    potential = chebyshev(first_box * shifted)
    to_first = -MIXING * potential * shifted
    to_second = -MIXING * jax.vmap(move)(potential * first_box, -offset_y, -offset_z)
    contrib = jnp.stack([to_first, to_second], axis=1).reshape(ref_count, planes * flat_cells)
    sending = jnp.dot(placed.astype(jnp.float32), contrib, precision=lax.Precision.HIGHEST)
    returned = lax.all_to_all(
        sending.reshape(n_orb, capacity, planes * flat_cells),
        "orb",
        split_axis=0,
        concat_axis=0,
        tiled=True,
    )
    owned = (asked.reshape(-1)[None, :] == jnp.arange(orb_dev, dtype=jnp.int32)[:, None]).astype(
        jnp.float32
    )
    exch_force = jnp.dot(
        owned,
        returned.reshape(n_orb * capacity, planes * flat_cells),
        precision=lax.Precision.HIGHEST,
    )
    rounded = exch_force.astype(jnp.bfloat16)
    own_rows = orbitals.reshape(orb_dev, planes * flat_cells)
    self_part = jnp.einsum("kc,kc->k", own_rows, rounded, preferred_element_type=jnp.float32)
    self_intersection = lax.psum(self_part, "grid") * BOX ** (-2.5)
    orbital_rows, force_rows = (
        lax.all_to_all(own_rows, "orb", split_axis=1, concat_axis=0, tiled=True),
        lax.all_to_all(rounded, "orb", split_axis=1, concat_axis=0, tiled=True),
    )
    intersection = lax.dot_general(
        orbital_rows, force_rows, (((1,), (1,)), ((), ())), preferred_element_type=jnp.float32
    )
    blocks = intersection.reshape(n_orb, orb_dev, n_orb, orb_dev).transpose(0, 2, 1, 3)
    blocks = blocks.reshape(n_orb * n_orb, orb_dev * orb_dev)
    picked = jnp.take(blocks, tiles[:, 0] * n_orb + tiles[:, 1], axis=0)
    summed = lax.psum_scatter(picked, ("grid", "orb"), scatter_dimension=0, tiled=True)
    return (
        exch_force.reshape(orb_dev, planes, flat_cells),
        summed * BOX ** (-1.5),
        self_intersection,
    )


def solution(mesh):
    in_specs = (P("orb", "grid", None), P("orb", None), P())
    out_specs = (P("orb", "grid", None), P(("grid", "orb"), None), P("orb"))
    return jax.shard_map(body, mesh=mesh, in_specs=in_specs, out_specs=out_specs, check_vma=False)
```

profile of v0, /device:TPU:0, one launch (start us, length us, event | category | flops | bytes accessed | tf_op | source)
XLA Modules:
  0.0 3068.2 jit_solution(2242388109963766361)
XLA Ops:
  2.3 14.3 all_to_all.57
  16.9 15.4 gather_fusion
  32.3 22.8 broadcast_select_fusion
  60.5 748.2 %all-to-all-done.1 = bf16[32,2,64,4096]{3,2,1,0:T(8,128)(2,1)} async-done(((bf16[32,2,64,4096]{3,2,1,0:T(8,128)(2,1)}), bf16[32,2,64,4096]{3,2,1,0:T(8,128)(2,1)}, u32[]{:S(2)}, u32[]{:S(2)}) %all-to-all-start.1) | async-done | bytes 33554464 | tf_op jit(solution)/shard_map/all_to_all | solution.py:89
  808.8 5.0 gather_fusion.1
  825.2 17.4 while.4
  852.6 4.9 fusion.66
  857.4 9.6 multiply_add_fusion.1
  873.5 4.9 fusion.63
  878.5 10.7 multiply_add_fusion
  889.1 4.9 fusion.59
  895.4 4.9 fusion.60
  900.4 19.9 multiply_bitcast_fusion.1
  930.0 17.9 while.5
  956.3 8.1 reshape.369
  964.4 41.6 %fusion.38 = f32[32,2,262144]{2,0,1:T(8,128)} fusion(f32[8,262144,1]{1,0,2:T(8,128)} %reshape.369, s32[32,2]{0,1:T(2,128)S(1)} %multiply_add_fusion.2, s32[8]{0:T(128)S(1)} %copy-done.10), kind=kOutput, calls=%fused_computation.85 | convolution fusion | flops 1610613248 | bytes 75497760 | tf_op jit(solution)/shard_map/dot_general | solution.py:101
  1006.0 107.7 %copy.52 = f32[32,2,262144]{2,1,0:T(2,128)} copy(f32[32,2,262144]{2,0,1:T(8,128)} %fusion.38) | data formatting | bytes 134217728 | tf_op jit(solution)/shard_map/dot_general | solution.py:101
  1113.7 5.1 all-to-all-start.2
  1118.8 13.0 all_to_all.48
  1131.9 11.2 copy.54
  1143.1 1480.7 %all-to-all-done.2 = f32[32,2,262144]{2,1,0:T(2,128)} async-done(((f32[32,2,262144]{2,1,0:T(2,128)}), f32[32,2,262144]{2,1,0:T(2,128)}, u32[]{:S(2)}, u32[]{:S(2)}) %all-to-all-start.2) | async-done | bytes 67108896 | tf_op jit(solution)/shard_map/all_to_all | solution.py:102
  2627.8 11.4 copy.65
  2640.5 99.2 %reshape.313 = f32[64,262144]{1,0:T(8,128)} reshape(f32[32,2,262144]{2,1,0:T(2,128)} %all-to-all-done.2) | data formatting | bytes 134217728 | tf_op jit(solution)/shard_map/reshape | solution.py:114
  2739.7 38.3 %fusion = (f32[16]{0:T(128)S(1)}, bf16[16,262144]{1,0:T(8,128)(2,1)}, f32[16,262144]{1,0:T(8,128)}) fusion(bf16[16,262144]{1,0:T(8,128)(2,1)} %bitcast.89, f32[64,262144]{1,0:T(8,128)} %reshape.313, s32[64]{0:T(128)S(1)} %eq.77), kind=kOutput, calls=%fused_computation.9 | convolution fusion | flops 3242198016 | bytes 100663616 | tf_op jit(solution)/shard_map/dot_general | solution.py:112
  2778.0 7.6 copy.67
  2785.6 28.2 all-to-all-done.4
  2817.7 17.8 copy.64
  2836.0 167.7 %all-to-all-done.3 = bf16[16,32,8192]{2,0,1:T(8,128)(2,1)} async-done(((bf16[16,32,8192]{2,0,1:T(8,128)(2,1)}), bf16[16,32,8192]{2,0,1:T(8,128)(2,1)}, u32[]{:S(2)}, u32[]{:S(2)}) %all-to-all-start.3) | async-done | bytes 8388640 | tf_op jit(solution)/shard_map/all_to_all | solution.py:123
  3003.7 9.5 convolution_bitcast_fusion
  3013.6 4.9 reshape.315
  3018.5 7.3 copy.56
  3030.5 36.9 %all-reduce.13 = f32[32,256]{1,0:T(8,128)S(1)} all-reduce(f32[32,256]{1,0:T(8,128)S(1)} %broadcast_select_fusion.2), channel_id=2, replica_groups=mesh['grid'=1,'orb'=32] {'grid','orb'}, use_global_device_ids=true, to_apply=%region_2.4.clone | all-reduce | flops 8192 | bytes 65536
  (118 shorter events, 105.3 us)
Async XLA Ops:
  1.6 0.5 copy-start.9
  16.6 15.7 copy-start.6
  55.2 4.5 copy-start.8
  55.2 753.6 %all-to-all-start.1 = ((bf16[32,2,64,4096]{3,2,1,0:T(8,128)(2,1)}), bf16[32,2,64,4096]{3,2,1,0:T(8,128)(2,1)}, u32[]{:S(2)}, u32[]{:S(2)}) async-start(bf16[32,2,64,4096]{3,2,1,0:T(8,128)(2,1)} %broadcast_select_fusion), calls=%async_computation.1 | async-start | bytes 67108864 | tf_op jit(solution)/shard_map/all_to_all | solution.py:89
  816.4 1.9 copy-start.4
  846.2 11.2 copy-start
  851.1 6.3 collective-permute-start
  851.8 5.7 copy-start.3
  851.8 5.7 collective-permute-start.1
  867.1 11.4 copy-start.1
  872.0 6.5 collective-permute-start.2
  872.6 5.8 collective-permute-start.3
  889.1 6.3 copy-start.2
  894.1 6.2 collective-permute-start.4
  894.8 5.6 collective-permute-start.5
  947.9 3.4 copy-start.5
  956.3 8.1 copy-start.10
  1113.7 1510.0 %all-to-all-start.2 = ((f32[32,2,262144]{2,1,0:T(2,128)}), f32[32,2,262144]{2,1,0:T(2,128)}, u32[]{:S(2)}, u32[]{:S(2)}) async-start(f32[32,2,262144]{2,1,0:T(2,128)} %copy.52), calls=%async_computation.2 | async-start | bytes 134217728 | tf_op jit(solution)/shard_map/all_to_all | solution.py:102
  2623.7 190.1 %all-to-all-start.4 = ((bf16[16,32,8192]{2,0,1:T(8,128)(2,1)}), bf16[16,32,8192]{2,0,1:T(8,128)(2,1)}, u32[]{:S(2)}, u32[]{:S(2)}) async-start(bf16[16,32,8192]{2,0,1:T(8,128)(2,1)} %copy.54), calls=%async_computation.4 | async-start | bytes 16777216 | tf_op jit(solution)/shard_map/all_to_all | solution.py:122
  2627.8 11.9 copy-start.7
  2813.8 3.9 copy-start.11
  2813.8 189.9 %all-to-all-start.3 = ((bf16[16,32,8192]{2,0,1:T(8,128)(2,1)}), bf16[16,32,8192]{2,0,1:T(8,128)(2,1)}, u32[]{:S(2)}, u32[]{:S(2)}) async-start(bf16[16,32,8192]{2,0,1:T(8,128)(2,1)} %bitcast.92), calls=%async_computation.3 | async-start | bytes 16777216 | tf_op jit(solution)/shard_map/all_to_all | solution.py:123
where the time goes:
time: 3080 us; the launch traced here: 3070 us
  waiting for transfers between devices  2420 us (79%)
  local copies, waits for them, and re-layouts  392 us (13%)
  matrix products  89.4 us (3%)
  other arithmetic  87.5 us (3%)
  blocking collectives  51.2 us (2%)
    all_to_all x1, waiting for transfers between devices, body(): lax.all_to_all(sending.reshape(n_orb, capacity, planes * flat_cells), 'or...  1480 us
    all_to_all x1, waiting for transfers between devices, body(): lax.all_to_all(outgoing, 'orb', split_axis=0, concat_axis=0, tiled=True)  748 us
    all_to_all x1, waiting for transfers between devices, body(): lax.all_to_all(rounded, 'orb', split_axis=1, concat_axis=0, tiled=True)  168 us
    dot_general x1, local copies, waits for them, and re-layouts, body(): jnp.dot(placed.astype(jnp.float32), contrib, precision=lax.Precision.HIGH...  108 us
    reshape x1, local copies, waits for them, and re-layouts, body(): returned.reshape(n_orb * capacity, planes * flat_cells)  99.2 us
  transfers between devices with their start and end apart: 10, of which 4 were waited for; matrix products, arithmetic and copies ran while one was open for 7% of the time, Pallas kernels for 0%

commit v1 on v0

--- a/solution.py
+++ b/solution.py
@@ -1,11 +1,17 @@
+import functools
+
 import jax
 import jax.numpy as jnp
+import numpy as np
 from jax import lax
+from jax.experimental import pallas as pl
+from jax.experimental.pallas import tpu as pltpu
 from jax.sharding import PartitionSpec as P
 
 BOX = 64
 SWEEPS = 3
-
+SHIFT = 16
+LANES = 128
 
 SCREENING = 0.02
 MIXING = 0.25
@@ -66,7 +72,7 @@
     return jnp.where(valid, rolled, 0.0)
 
 
-def body(orbitals, pairs, tiles):
+def general_body(orbitals, pairs, tiles):
     n_orb = lax.axis_size("orb")
     orb_dev, planes, flat_cells = orbitals.shape
     pair_count = pairs.shape[0]
@@ -136,6 +142,226 @@
     )
 
 
+def polynomial():
+    center = 6.0 + SCREENING
+    radius = 6.0
+    ratio = center / radius
+    residual = np.zeros(SWEEPS + 1)
+    residual[0] = 1.0
+    direction = residual / center
+    total = direction.copy()
+    previous = 1.0 / ratio
+    for _ in range(SWEEPS):
+        moved = np.concatenate([[0.0], direction[:-1]])
+        residual = residual - (center * direction - moved)
+        current = 1.0 / (2.0 * ratio - previous)
+        direction = current * previous * direction + 2.0 * current / radius * residual
+        total = total + direction
+        previous = current
+    return [-MIXING * float(value) for value in total]
+
+
+def chain(n_orb):
+    if n_orb % 8:
+        return list(range(n_orb))
+    order = []
+    for layer in range(n_orb // 8):
+        ring = [0, 1, 3, 2]
+        for chip in ring if layer % 2 == 0 else ring[::-1]:
+            order += [(layer * 4 + chip) * 2, (layer * 4 + chip) * 2 + 1]
+    return order
+
+
+PAD = 16
+
+
+def shift_cells(field_in, offset_y, offset_z, pad):
+    planes, rows, lanes = field_in.shape
+    step = offset_y * BOX + offset_z
+    down = lax.shift_right_arithmetic(step, jnp.int32(7))
+    along = step - down * lanes
+    turned = pltpu.roll(field_in.reshape(planes * rows, lanes), lax.rem(lanes - along, lanes), 1)
+    pad[:, PAD:PAD + rows, :] = turned.reshape(planes, rows, lanes)
+    near = pad[:, pl.ds(PAD + down, rows), :]
+    far = pad[:, pl.ds(PAD + 1 + down, rows), :]
+    lane = lax.broadcasted_iota(jnp.int32, (rows, lanes), 1)
+    column = lax.rem(lane, BOX) + offset_z
+    valid = (column >= 0) & (column < BOX)
+    keep = valid & (lane < lanes - along)
+    other = valid & (lane >= lanes - along)
+    return jnp.where(keep[None], near, jnp.where(other[None], far, 0.0))
+
+
+def density_kernel(refs, slab, out, pad):
+    pad[...] = jnp.zeros_like(pad)
+
+    def pair(p, carry):
+        first = slab[refs[p, 0]].astype(jnp.float32)
+        second = slab[refs[p, 1]].astype(jnp.float32)
+        out[p] = (first * shift_cells(second, refs[p, 2], refs[p, 3], pad)).astype(out.dtype)
+        return carry
+
+    lax.fori_loop(0, out.shape[0], pair, 0)
+
+
+def force_kernel(n_orb, before, coefficients, refs, place, slab, *rest):
+    sides = rest[:-4]
+    rounded, forces, pad, pad_back = rest[-4:]
+    orbitals, planes, rows, lanes = slab.shape
+    pad[...] = jnp.zeros_like(pad)
+    pad_back[...] = jnp.zeros_like(pad_back)
+
+    def clear(k, carry):
+        forces[k] = jnp.zeros(forces.shape[1:], jnp.float32)
+        return carry
+
+    lax.fori_loop(0, orbitals, clear, 0)
+    first_plane = place[0] * planes
+    lane = lax.broadcasted_iota(jnp.int32, (rows, lanes), 1)
+    row = lax.broadcasted_iota(jnp.int32, (rows, lanes), 0)
+    low_half = lane < BOX
+    column = lax.rem(lane, BOX)
+    not_last = column < BOX - 1
+    not_first = column > 0
+    inner = jnp.where(low_half, jnp.where(row > 0, 1.0, 0.0), jnp.where(row < rows - 1, 1.0, 0.0))
+    inside = []
+    for k in range(planes + 2 * SWEEPS):
+        x = first_plane + (k - SWEEPS)
+        inside.append(jnp.where((x >= 0) & (x < n_orb * planes), 1.0, 0.0).astype(jnp.float32))
+
+    def in_plane(field_in):
+        swapped = pltpu.roll(field_in, BOX, 1)
+        across = jnp.where(low_half, pltpu.roll(swapped, 1, 0), pltpu.roll(swapped, rows - 1, 0))
+        upward = jnp.where(not_last, pltpu.roll(field_in, lanes - 1, 1), 0.0)
+        downward = jnp.where(not_first, pltpu.roll(field_in, 1, 1), 0.0)
+        return swapped + across * inner + upward + downward
+
+    def pair(p, carry):
+        first_at, second_at, offset_y, offset_z = refs[p, 0], refs[p, 1], refs[p, 2], refs[p, 3]
+        first = slab[first_at].astype(jnp.float32)
+        shifted = shift_cells(slab[second_at].astype(jnp.float32), offset_y, offset_z, pad)
+        own = first * shifted
+        density = []
+        for ref, plane in before[0]:
+            density.append(sides[ref][p, plane].astype(jnp.float32))
+        density += [own[k] for k in range(planes)]
+        for ref, plane in before[1]:
+            density.append(sides[ref][p, plane].astype(jnp.float32))
+        field = [coefficients[SWEEPS] * d for d in density]
+        for sweep in range(SWEEPS):
+            factor = coefficients[SWEEPS - 1 - sweep]
+            low, high = sweep + 1, planes + 2 * SWEEPS - 1 - sweep
+            after = [None] * len(field)
+            for k in range(low, high):
+                value = factor * density[k] + (field[k - 1] + field[k + 1] + in_plane(field[k]))
+                if k < SWEEPS or k >= SWEEPS + planes:
+                    value = value * inside[k]
+                after[k] = value
+            field = after
+        potential = jnp.stack(field[SWEEPS:SWEEPS + planes])
+        forces[first_at] += potential * shifted
+        forces[second_at] += shift_cells(potential * first, -offset_y, -offset_z, pad_back)
+        return carry
+
+    lax.fori_loop(0, refs.shape[0], pair, 0)
+
+    def finish(k, carry):
+        rounded[k] = forces[k].astype(rounded.dtype)
+        return carry
+
+    lax.fori_loop(0, orbitals, finish, 0)
+
+
+def slab_body(orbitals, pairs, tiles):
+    n_orb = lax.axis_size("orb")
+    orb_dev, box_planes, flat_cells = orbitals.shape
+    planes = box_planes // n_orb
+    rows = flat_cells // LANES
+    n_orbitals = n_orb * orb_dev
+    order = chain(n_orb)
+    position = [order.index(d) for d in range(n_orb)]
+    groups = [order]
+    exchange = functools.partial(
+        lax.all_to_all, axis_name="orb", split_axis=0, concat_axis=0, tiled=True,
+        axis_index_groups=groups,
+    )
+    seat = jnp.asarray(position, jnp.int32)
+    me = lax.axis_index("orb")
+
+    leaving = orbitals.reshape(orb_dev, n_orb, planes, rows, LANES).transpose(1, 0, 2, 3, 4)
+    slab = exchange(leaving).reshape(n_orbitals, planes, rows, LANES)
+    every = exchange(jnp.broadcast_to(pairs[None], (n_orb,) + pairs.shape)).reshape(-1, 4)
+    ids = every[:, :2]
+    slots = jnp.take(seat, ids // orb_dev) * orb_dev + ids % orb_dev
+    refs = jnp.concatenate([slots, every[:, 2:]], axis=1)
+    n_pairs = refs.shape[0]
+
+    vmem = pl.BlockSpec(memory_space=pltpu.VMEM)
+    smem = pl.BlockSpec(memory_space=pltpu.SMEM)
+    limit = pltpu.CompilerParams(vmem_limit_bytes=60 * 1024 * 1024)
+    pad = pltpu.VMEM((planes, rows + 2 * PAD, LANES), jnp.float32)
+    density = pl.pallas_call(
+        density_kernel,
+        out_shape=jax.ShapeDtypeStruct((n_pairs, planes, rows, LANES), jnp.bfloat16),
+        in_specs=[smem, vmem],
+        out_specs=vmem,
+        scratch_shapes=[pad],
+        compiler_params=limit,
+    )(refs, slab)
+
+    sides, lower, upper = [], [], []
+    left = SWEEPS
+    hop = 1
+    while left > 0:
+        width = min(planes, left)
+        up = [(order[s], order[s + hop]) for s in range(n_orb - hop)]
+        down = [(j, i) for i, j in up]
+        sides.append(lax.ppermute(density[:, planes - width:], "orb", up))
+        lower = [(len(sides) - 1, k) for k in range(width)] + lower
+        sides.append(lax.ppermute(density[:, :width], "orb", down))
+        upper = upper + [(len(sides) - 1, k) for k in range(width)]
+        left -= width
+        hop += 1
+
+    rounded = pl.pallas_call(
+        functools.partial(force_kernel, n_orb, (lower, upper), polynomial()),
+        out_shape=jax.ShapeDtypeStruct((n_orbitals, planes, rows, LANES), jnp.bfloat16),
+        in_specs=[smem, smem, vmem] + [vmem] * len(sides),
+        out_specs=vmem,
+        scratch_shapes=[
+            pltpu.VMEM((n_orbitals, planes, rows, LANES), jnp.float32), pad, pad,
+        ],
+        compiler_params=limit,
+    )(refs, jnp.take(seat, me).reshape(1), slab, *sides)
+
+    returned = exchange(rounded.reshape(n_orb, orb_dev, planes, rows, LANES))
+    exch_force = returned.astype(jnp.float32).transpose(1, 0, 2, 3, 4)
+    exch_force = exch_force.reshape(orb_dev, box_planes, flat_cells)
+
+    intersection = lax.dot_general(
+        slab.reshape(n_orbitals, -1), rounded.reshape(n_orbitals, -1),
+        (((1,), (1,)), ((), ())), preferred_element_type=jnp.float32,
+    )
+    self_part = jnp.diagonal(intersection).reshape(n_orb, orb_dev)
+    blocks = intersection.reshape(n_orb, orb_dev, n_orb, orb_dev).transpose(0, 2, 1, 3)
+    blocks = blocks.reshape(n_orb * n_orb, orb_dev * orb_dev)
+    chosen = jnp.take(seat, tiles[:, 0]) * n_orb + jnp.take(seat, tiles[:, 1])
+    picked = jnp.take(blocks, chosen, axis=0).reshape(n_orb, -1)
+    parts = jnp.concatenate([jnp.take(picked, np.asarray(order), axis=0), self_part], axis=1)
+    summed = jnp.sum(exchange(parts), axis=0)
+    width = picked.shape[1]
+    tile_rows = summed[:width].reshape(-1, orb_dev * orb_dev)
+    return exch_force, tile_rows * BOX ** (-1.5), summed[width:] * BOX ** (-2.5)
+
+
+def body(orbitals, pairs, tiles):
+    planes, flat_cells = orbitals.shape[1:]
+    n_orb = lax.axis_size("orb")
+    if lax.axis_size("grid") == 1 and planes % n_orb == 0 and flat_cells % LANES == 0:
+        return slab_body(orbitals, pairs, tiles)
+    return general_body(orbitals, pairs, tiles)
+
+
 def solution(mesh):
     in_specs = (P("orb", "grid", None), P("orb", None), P())
     out_specs = (P("orb", "grid", None), P(("grid", "orb"), None), P("orb"))

time: 3080 us -> 649 us (0.21)
  waiting for transfers between devices: 2420 us -> 396 us
  local copies, waits for them, and re-layouts: 392 us -> 95.5 us
  Pallas kernels: 0 us -> 89.2 us
  matrix products: 89.4 us -> 14.8 us
  other arithmetic: 87.5 us -> 14 us
  blocking collectives: 51.2 us -> 11 us
    all_to_all x4 -> x3, waiting for transfers between devices: 2420 us -> 372 us  [the longest x1 187 us: slab_body(): returned = exchange(rounded.reshape(n_orb, orb_dev, planes, rows, LANES))]
    dot_general x2 -> x1, local copies, waits for them, and re-layouts: 108 us -> 0.33 us  [slab_body(): lax.dot_general(slab.reshape(n_orbitals, -1), rounded.reshape(n_orbitals,...]
    pallas_call x0 -> x2, Pallas kernels: none -> 89.2 us  [the longest x1 72.8 us: slab_body(): pl.pallas_call(functools.partial(force_kernel, n_orb, (lower, upper), pol...]
    dot_general x3 -> x1, matrix products: 89.4 us -> 14.8 us  [slab_body(): lax.dot_general(slab.reshape(n_orbitals, -1), rounded.reshape(n_orbitals,...]
    reshape x8 -> x7, local copies, waits for them, and re-layouts: 117 us -> 49.1 us  [the longest x2 30.5 us: slab_body(): exch_force = exch_force.reshape(orb_dev, box_planes, flat_cells)]
    unnamed x1 -> x0, blocking collectives: 36.9 us -> none
    all_to_all x6 -> x1, local copies, waits for them, and re-layouts: 32.6 us -> 0.05 us  [slab_body(): summed = jnp.sum(exchange(parts), axis=0)]
  transfers between devices with their start and end apart: 10 -> 7, of which waited for: 4 -> 4; matrix products, arithmetic and copies ran while one was open for 7% -> 6% of each run, Pallas kernels for 0% -> 0%
where the time goes in v1:
time: 649 us; the launch traced here: 648 us
  waiting for transfers between devices  396 us (61%)
  local copies, waits for them, and re-layouts  95.5 us (15%)
  Pallas kernels  89.2 us (14%)
  starting transfers between devices  25.6 us (4%)
  matrix products  14.8 us (2%)
  other arithmetic  14 us (2%)
  blocking collectives  11 us (2%)
    all_to_all x1, waiting for transfers between devices, slab_body(): returned = exchange(rounded.reshape(n_orb, orb_dev, planes, rows, LANES))  187 us
    all_to_all x1, waiting for transfers between devices, slab_body(): slab = exchange(leaving).reshape(n_orbitals, planes, rows, LANES)  185 us
    pallas_call x1, Pallas kernels, slab_body(): pl.pallas_call(functools.partial(force_kernel, n_orb, (lower, upper), pol...  72.8 us
    reshape x2, local copies, waits for them, and re-layouts, slab_body(): exch_force = exch_force.reshape(orb_dev, box_planes, flat_cells)  30.5 us
    ppermute x2, waiting for transfers between devices, slab_body(): sides.append(lax.ppermute(density[:, :width], 'orb', down))  17.8 us
    pallas_call x1, Pallas kernels, slab_body(): pl.pallas_call(density_kernel, out_shape=jax.ShapeDtypeStruct((n_pairs, p...  16.4 us
    dot_general x1, matrix products, slab_body(): lax.dot_general(slab.reshape(n_orbitals, -1), rounded.reshape(n_orbitals,...  14.8 us
    another operation x1, local copies, waits for them, and re-layouts, slab_body(): slab.reshape(n_orbitals, -1)  13.3 us
  transfers between devices with their start and end apart: 7, of which 4 were waited for; matrix products, arithmetic and copies ran while one was open for 6% of the time, Pallas kernels for 0%

profile of v1, /device:TPU:0, one launch (start us, length us, event | category | flops | bytes accessed | tf_op | source)
XLA Modules:
  0.0 647.8 jit_solution(8999960767714461827)
XLA Ops:
  0.6 1.3 broadcast_in_dim.50
  2.0 7.3 %all-to-all-start = ((s32[32,4,4]{2,1,0:T(4,128)}), s32[32,4,4]{2,1,0:T(4,128)S(1)}, u32[]{:S(2)}, u32[]{:S(2)}) async-start(s32[32,4,4]{2,1,0:T(4,128)} %broadcast_in_dim.50), calls=%async_computation | async-start | bytes 131072 | tf_op jit(solution)/shard_map/all_to_all | solution.py:293
  9.3 9.6 %copy.33 = bf16[128,8,32,128]{3,2,1,0:T(8,128)(2,1)} copy(bf16[128,8,32,128]{3,1,2,0:T(8,128)(2,1)} %bitcast.52) | data formatting | bytes 16777216
  18.9 9.6 %copy.42 = bf16[16,32,2,32,128]{4,3,2,0,1:T(8,128)(2,1)} copy(bf16[16,32,2,32,128]{4,3,2,1,0:T(8,128)(2,1)} %bitcast.51) | data formatting | bytes 16777216 | tf_op jit(solution)/shard_map/reshape | solution.py:291
  28.5 6.0 all-to-all-start.1
  34.7 1.9 gather_fusion
  36.9 0.7 pad_add_fusion.refs
  37.6 185.2 %all-to-all-done.1 = bf16[32,16,2,32,128]{4,3,2,1,0:T(8,128)(2,1)} async-done(((bf16[32,16,2,32,128]{4,3,2,1,0:T(8,128)(2,1)}), bf16[32,16,2,32,128]{4,3,2,1,0:T(8,128)(2,1)}, u32[]{:S(2)}, u32[]{:S(2)}) %all-to-all-start.1) | async-done | bytes 8388640 | tf_op jit(solution)/shard_map/all_to_all | solution.py:292
  222.7 16.4 %shard_map.76 = bf16[128,2,32,128]{3,2,1,0:T(8,128)(2,1)} custom-call(s32[128,4]{1,0:T(8,128)} %pad_add_fusion.refs, bf16[512,2,32,128]{3,2,1,0:T(8,128)(2,1)} %bitcast.3.slab), custom_call_target="tpu_custom_call" | custom-call | tf_op jit(solution)/shard_map/pallas_call | solution.py:303
  239.2 1.6 collective-permute-start
  240.7 1.3 collective-permute-start.1
  242.0 3.3 fusion.10
  245.3 4.1 collective-permute-start.2
  249.4 1.5 collective-permute-start.3
  251.5 0.7 gather_fusion.4
  252.2 0.7 gather_fusion.5
  253.6 13.3 %reshape_reshape.3 = bf16[512,8192]{1,0:T(8,128)(2,1)} reshape(bf16[32,16,2,32,128]{4,3,2,1,0:T(8,128)(2,1)} %all-to-all-done.1) | data formatting | bytes 16777216 | tf_op jit(solution)/shard_map/reshape;reshape | solution.py:342
  266.9 6.2 collective-permute-done.2.rest_2_
  273.2 17.8 %collective-permute-done.3.rest_3_ = bf16[128,1,32,128]{3,2,1,0:T(8,128)(2,1)} collective-permute-done((bf16[128,1,32,128]{3,2,1,0:T(8,128)(2,1)}, bf16[128,1,32,128]{3,2,1,0:T(8,128)(2,1)}, u32[]{:S(2)}, u32[]{:S(2)}) %collective-permute-start.3) | collective-permute-done | bytes 1048608 | tf_op jit(solution)/shard_map/ppermute | solution.py:321
  291.0 1.3 copy-done.1
  292.3 72.8 %shard_map.77 = bf16[512,2,32,128]{3,2,1,0:T(8,128)(2,1)} custom-call(s32[128,4]{1,0:T(8,128)} %pad_add_fusion.refs, s32[1]{0:T(128)S(6)} %select_n.68.place, bf16[512,2,32,128]{3,2,1,0:T(8,128)(2,1)} %bitcast.3.slab, bf16[128,2,32,128]{3,2,1,0:T(8,128)(2,1)} %copy-done.1, bf16[128,2,32,128]{3,2,1,0:T(8,128)(2,1)} %collective-permute-done.1.rest_1_, ...), custom_call_target="tpu_custom_call" | custom-call | tf_op jit(solution)/shard_map/pallas_call | solution.py:326
  365.1 14.8 %fusion.3 = f32[512,512]{0,1:T(8,128)S(1)} fusion(bf16[512,8192]{1,0:T(8,128)(2,1)} %reshape_reshape.3, bf16[64,8,64,128]{3,2,1,0:T(8,128)(2,1)} %bitcast.47), kind=kOutput, calls=%fused_computation.11 | convolution fusion | flops 4294967296 | bytes 17825792 | tf_op jit(solution)/shard_map/dot_general | solution.py:341
  380.2 4.9 reshape.73
  385.1 7.2 %copy.30 = f32[32,32,16,16]{1,0,3,2:T(8,128)} copy(f32[32,32,16,16]{3,1,2,0:T(8,128)} %bitcast.49) | data formatting | bytes 2097152 | tf_op jit(solution)/shard_map/transpose | solution.py:346
  392.3 3.7 reshape.74
  396.4 4.5 gather_fusion.3
  402.4 11.0 %all_to_all.24 = f32[32,1,272]{2,1,0:T(1,128)S(1)} all-to-all(f32[32,1,272]{2,1,0:T(1,128)S(1)} %copy.32), channel_id=1, replica_groups={{0,1,2,3,6,7,4,5,12,13,14,15,10,11,8,9,16,17,18,19,22,23,20,21,28,29,30..., dimensions={0} | all-to-all | bytes 69632 | tf_op jit(solution)/shard_map/all_to_all | solution.py:351
  413.4 3.9 all-to-all-start.2
  418.4 187.0 %all-to-all-done.2 = bf16[32,16,2,32,128]{4,3,2,1,0:T(8,128)(2,1)} async-done(((bf16[32,16,2,32,128]{4,3,2,1,0:T(8,128)(2,1)}), bf16[32,16,2,32,128]{4,3,2,1,0:T(8,128)(2,1)}, u32[]{:S(2)}, u32[]{:S(2)}) %all-to-all-start.2) | async-done | bytes 8388640 | tf_op jit(solution)/shard_map/all_to_all | solution.py:337
  605.5 11.9 %convert_bitcast_fusion = f32[16,32,2,32,128]{4,3,2,0,1:T(8,128)} fusion(bf16[32,16,2,32,128]{4,3,2,1,0:T(8,128)(2,1)} %all-to-all-done.2), kind=kLoop, calls=%fused_computation.6 | loop fusion | flops 4194304 | bytes 25165824 | tf_op jit(solution)/shard_map/reshape | solution.py:339
  617.4 12.3 %copy.28 = f32[16,32,2,32,128]{4,3,2,1,0:T(8,128)} copy(f32[16,32,2,32,128]{4,3,2,0,1:T(8,128)} %convert_bitcast_fusion) | data formatting | bytes 33554432 | tf_op jit(solution)/shard_map/reshape | solution.py:339
  629.6 18.2 %reshape.107 = f32[16,64,4096]{2,1,0:T(8,128)} reshape(f32[16,32,2,32,128]{4,3,2,1,0:T(8,128)} %copy.28) | data formatting | bytes 33554432 | tf_op jit(solution)/shard_map/reshape | solution.py:339
  (35 shorter events, 4.3 us)
Async XLA Ops:
  2.0 26.6 %all-to-all-start = ((s32[32,4,4]{2,1,0:T(4,128)}), s32[32,4,4]{2,1,0:T(4,128)S(1)}, u32[]{:S(2)}, u32[]{:S(2)}) async-start(s32[32,4,4]{2,1,0:T(4,128)} %broadcast_in_dim.50), calls=%async_computation | async-start | bytes 131072 | tf_op jit(solution)/shard_map/all_to_all | solution.py:293
  28.5 6.2 copy-start
  28.5 194.2 %all-to-all-start.1 = ((bf16[32,16,2,32,128]{4,3,2,1,0:T(8,128)(2,1)}), bf16[32,16,2,32,128]{4,3,2,1,0:T(8,128)(2,1)}, u32[]{:S(2)}, u32[]{:S(2)}) async-start(bf16[32,16,2,32,128]{4,3,2,1,0:T(8,128)(2,1)} %bitcast.50), calls=%async_computation.1 | async-start | bytes 16777216 | tf_op jit(solution)/shard_map/all_to_all | solution.py:292
  36.6 214.9 %copy-start.3 = (s32[32,2]{0,1:T(2,128)S(1)}, s32[32,2]{0,1:T(2,128)}, u32[]{:S(2)}) copy-start(s32[32,2]{0,1:T(2,128)} %param.9) | copy-start | bytes 772
  36.6 217.0 %copy-start.4 = (s32[32]{0:T(128)S(1)}, s32[32]{0:T(128)}, u32[]{:S(2)}) copy-start(s32[32]{0:T(128)} %constant.169) | copy-start | bytes 388
  239.2 51.8 %collective-permute-start = (bf16[128,2,32,128]{3,2,1,0:T(8,128)(2,1)}, bf16[128,2,32,128]{3,2,1,0:T(8,128)(2,1)S(1)}, u32[]{:S(2)}, u32[]{:S(2)}) collective-permute-start(bf16[128,2,32,128]{3,2,1,0:T(8,128)(2,1)} %shard_map.76), channel_id=1, source_target_pairs={{0,1},{1,2},{2,3},{3,6},{6,7},{7,4},{4,5},{5,12},{12,13},{13,14},{... | collective-permute-start | bytes 6291464 | tf_op jit(solution)/shard_map/ppermute | solution.py:319
  240.7 50.2 %collective-permute-start.1 = (bf16[128,2,32,128]{3,2,1,0:T(8,128)(2,1)}, bf16[128,2,32,128]{3,2,1,0:T(8,128)(2,1)}, u32[]{:S(2)}, u32[]{:S(2)}) collective-permute-start(bf16[128,2,32,128]{3,2,1,0:T(8,128)(2,1)} %shard_map.76), channel_id=1, source_target_pairs={{1,0},{2,1},{3,2},{6,3},{7,6},{4,7},{5,4},{12,5},{13,12},{14,13},{... | collective-permute-start | bytes 6291464 | tf_op jit(solution)/shard_map/ppermute | solution.py:321
  245.3 27.9 %collective-permute-start.2 = (bf16[128,1,32,128]{3,2,1,0:T(8,128)(2,1)}, bf16[128,1,32,128]{3,2,1,0:T(8,128)(2,1)S(1)}, u32[]{:S(2)}, u32[]{:S(2)}) collective-permute-start(bf16[128,1,32,128]{3,2,1,0:T(8,128)(2,1)} %get-tuple-element.29), channel_id=1, source_target_pairs={{0,2},{1,3},{2,6},{3,7},{6,4},{7,5},{4,12},{5,13},{12,14},{13,15},... | collective-permute-start | bytes 3145736 | tf_op jit(solution)/shard_map/ppermute | solution.py:319
  249.4 41.6 %collective-permute-start.3 = (bf16[128,1,32,128]{3,2,1,0:T(8,128)(2,1)}, bf16[128,1,32,128]{3,2,1,0:T(8,128)(2,1)}, u32[]{:S(2)}, u32[]{:S(2)}) collective-permute-start(bf16[128,1,32,128]{3,2,1,0:T(8,128)(2,1)} %get-tuple-element.28), channel_id=1, source_target_pairs={{2,0},{3,1},{6,2},{7,3},{4,6},{5,7},{12,4},{13,5},{14,12},{15,13},... | collective-permute-start | bytes 3145736 | tf_op jit(solution)/shard_map/ppermute | solution.py:321
  273.2 17.8 %copy-start.2 = (bf16[128,1,32,128]{3,2,1,0:T(8,128)(2,1)}, bf16[128,1,32,128]{3,2,1,0:T(8,128)(2,1)S(1)}, u32[]{:S(2)}) copy-start(bf16[128,1,32,128]{3,2,1,0:T(8,128)(2,1)S(1)} %collective-permute-done.2.rest_2_) | copy-start | bytes 3145732
  290.9 1.3 copy-start.1
  413.4 192.1 %all-to-all-start.2 = ((bf16[32,16,2,32,128]{4,3,2,1,0:T(8,128)(2,1)}), bf16[32,16,2,32,128]{4,3,2,1,0:T(8,128)(2,1)}, u32[]{:S(2)}, u32[]{:S(2)}) async-start(bf16[32,16,2,32,128]{4,3,2,1,0:T(8,128)(2,1)} %bitcast.48), calls=%async_computation.2 | async-start | bytes 16777216 | tf_op jit(solution)/shard_map/all_to_all | solution.py:337

commit v2 on v1

--- a/solution.py
+++ b/solution.py
@@ -1,4 +1,5 @@
 import functools
+import math
 
 import jax
 import jax.numpy as jnp
@@ -192,30 +193,68 @@
     return jnp.where(keep[None], near, jnp.where(other[None], far, 0.0))
 
 
-def density_kernel(refs, slab, out, pad):
-    pad[...] = jnp.zeros_like(pad)
-
-    def pair(p, carry):
-        first = slab[refs[p, 0]].astype(jnp.float32)
-        second = slab[refs[p, 1]].astype(jnp.float32)
-        out[p] = (first * shift_cells(second, refs[p, 2], refs[p, 3], pad)).astype(out.dtype)
+def density_kernel(refs, slab, out, pads):
+    pads[...] = jnp.zeros_like(pads)
+    width = pads.shape[0]
+
+    def group(g, carry):
+        values = []
+        for u in range(width):
+            p = g * width + u
+            first = slab[refs[p, 0]].astype(jnp.float32)
+            second = slab[refs[p, 1]].astype(jnp.float32)
+            values.append(first * shift_cells(second, refs[p, 2], refs[p, 3], pads.at[u]))
+        for u in range(width):
+            out[g * width + u] = values[u].astype(out.dtype)
         return carry
 
-    lax.fori_loop(0, out.shape[0], pair, 0)
-
-
-def force_kernel(n_orb, before, coefficients, refs, place, slab, *rest):
-    sides = rest[:-4]
-    rounded, forces, pad, pad_back = rest[-4:]
+    lax.fori_loop(0, out.shape[0] // width, group, 0)
+
+
+def spread_kernel(own, out, lines):
+    box_planes, flat_cells = own.shape[1:]
+    slabs, _, planes, rows, lanes = out.shape
+    for r in range(rows):
+        lines[pl.ds(r, box_planes, stride=rows), :] = own[0, :, r * lanes:(r + 1) * lanes].astype(
+            jnp.float32
+        )
+    out[...] = lines[...].reshape(out.shape).astype(out.dtype)
+
+
+def collect_kernel(back, out, lines):
+    box_planes, flat_cells = out.shape[1:]
+    slabs, _, planes, rows, lanes = back.shape
+    lines[...] = back[...].astype(jnp.float32).reshape(lines.shape)
+    for r in range(rows):
+        out[0, :, r * lanes:(r + 1) * lanes] = lines[pl.ds(r, box_planes, stride=rows), :]
+
+
+def force_kernel(n_orb, before, coefficients, last, refs, place, slab, *rest):
+    if last:
+        sides = rest[:-6]
+        all_refs, earlier, rounded, forces, pads, pads_back = rest[-6:]
+    else:
+        sides = rest[:-3]
+        given, pads, pads_back = rest[-3:]
     orbitals, planes, rows, lanes = slab.shape
-    pad[...] = jnp.zeros_like(pad)
-    pad_back[...] = jnp.zeros_like(pad_back)
-
-    def clear(k, carry):
-        forces[k] = jnp.zeros(forces.shape[1:], jnp.float32)
-        return carry
-
-    lax.fori_loop(0, orbitals, clear, 0)
+    width = pads.shape[0]
+    pads[...] = jnp.zeros_like(pads)
+    pads_back[...] = jnp.zeros_like(pads_back)
+
+    if last:
+        def clear(k, carry):
+            forces[k] = jnp.zeros(forces.shape[1:], jnp.float32)
+            return carry
+
+        lax.fori_loop(0, orbitals, clear, 0)
+
+        def add(p, carry):
+            forces[all_refs[p, 0]] += earlier[p, 0]
+            forces[all_refs[p, 1]] += earlier[p, 1]
+            return carry
+
+        lax.fori_loop(0, earlier.shape[0], add, 0)
+
     first_plane = place[0] * planes
     lane = lax.broadcasted_iota(jnp.int32, (rows, lanes), 1)
     row = lax.broadcasted_iota(jnp.int32, (rows, lanes), 0)
@@ -236,7 +275,7 @@
         downward = jnp.where(not_first, pltpu.roll(field_in, 1, 1), 0.0)
         return swapped + across * inner + upward + downward
 
-    def pair(p, carry):
+    def contributions(p, pad, pad_back):
         first_at, second_at, offset_y, offset_z = refs[p, 0], refs[p, 1], refs[p, 2], refs[p, 3]
         first = slab[first_at].astype(jnp.float32)
         shifted = shift_cells(slab[second_at].astype(jnp.float32), offset_y, offset_z, pad)
@@ -259,17 +298,47 @@
                 after[k] = value
             field = after
         potential = jnp.stack(field[SWEEPS:SWEEPS + planes])
-        forces[first_at] += potential * shifted
-        forces[second_at] += shift_cells(potential * first, -offset_y, -offset_z, pad_back)
+        moved = shift_cells(potential * first, -offset_y, -offset_z, pad_back)
+        return potential * shifted, moved
+
+    def group(g, carry):
+        pieces = []
+        for u in range(width):
+            pieces.append(contributions(g * width + u, pads.at[u], pads_back.at[u]))
+        for u in range(width):
+            p = g * width + u
+            if last:
+                forces[refs[p, 0]] += pieces[u][0]
+                forces[refs[p, 1]] += pieces[u][1]
+            else:
+                given[p, 0] = pieces[u][0]
+                given[p, 1] = pieces[u][1]
         return carry
 
-    lax.fori_loop(0, refs.shape[0], pair, 0)
-
-    def finish(k, carry):
-        rounded[k] = forces[k].astype(rounded.dtype)
-        return carry
-
-    lax.fori_loop(0, orbitals, finish, 0)
+    lax.fori_loop(0, refs.shape[0] // width, group, 0)
+
+    if last:
+        def finish(k, carry):
+            rounded[k] = forces[k].astype(rounded.dtype)
+            return carry
+
+        lax.fori_loop(0, orbitals, finish, 0)
+
+
+def reduce_parts(parts, n_orb, me):
+    if n_orb & (n_orb - 1):
+        return jnp.sum(
+            lax.all_to_all(parts, "orb", split_axis=0, concat_axis=0, tiled=True), axis=0
+        )
+    bit = n_orb // 2
+    while bit:
+        upper = (me & bit) != 0
+        low, high = parts[:bit], parts[bit:]
+        sent = jnp.where(upper, low, high)
+        kept = jnp.where(upper, high, low)
+        parts = kept + lax.ppermute(sent, "orb", [(d, d ^ bit) for d in range(n_orb)])
+        bit //= 2
+    return parts
 
 
 def slab_body(orbitals, pairs, tiles):
@@ -288,7 +357,14 @@
     seat = jnp.asarray(position, jnp.int32)
     me = lax.axis_index("orb")
 
-    leaving = orbitals.reshape(orb_dev, n_orb, planes, rows, LANES).transpose(1, 0, 2, 3, 4)
+    leaving = pl.pallas_call(
+        spread_kernel,
+        grid=(orb_dev,),
+        out_shape=jax.ShapeDtypeStruct((n_orb, orb_dev, planes, rows, LANES), orbitals.dtype),
+        in_specs=[pl.BlockSpec((1, box_planes, flat_cells), lambda k: (k, 0, 0))],
+        out_specs=pl.BlockSpec((n_orb, 1, planes, rows, LANES), lambda k: (0, k, 0, 0, 0)),
+        scratch_shapes=[pltpu.VMEM((box_planes * rows, LANES), jnp.float32)],
+    )(orbitals)
     slab = exchange(leaving).reshape(n_orbitals, planes, rows, LANES)
     every = exchange(jnp.broadcast_to(pairs[None], (n_orb,) + pairs.shape)).reshape(-1, 4)
     ids = every[:, :2]
@@ -298,45 +374,85 @@
 
     vmem = pl.BlockSpec(memory_space=pltpu.VMEM)
     smem = pl.BlockSpec(memory_space=pltpu.SMEM)
-    limit = pltpu.CompilerParams(vmem_limit_bytes=60 * 1024 * 1024)
-    pad = pltpu.VMEM((planes, rows + 2 * PAD, LANES), jnp.float32)
-    density = pl.pallas_call(
-        density_kernel,
-        out_shape=jax.ShapeDtypeStruct((n_pairs, planes, rows, LANES), jnp.bfloat16),
-        in_specs=[smem, vmem],
+    limit = pltpu.CompilerParams(vmem_limit_bytes=58 * 1024 * 1024)
+    chunks = 2 if n_pairs % 8 == 0 else 1
+    chunk = n_pairs // chunks
+    group = math.gcd(chunk, 4)
+    pair_group = math.gcd(chunk, 2)
+
+    def pads(count):
+        return pltpu.VMEM((count, planes, rows + 2 * PAD, LANES), jnp.float32)
+
+    def density_of(chunk_refs):
+        return pl.pallas_call(
+            density_kernel,
+            out_shape=jax.ShapeDtypeStruct((chunk, planes, rows, LANES), jnp.bfloat16),
+            in_specs=[smem, vmem],
+            out_specs=vmem,
+            scratch_shapes=[pads(group)],
+            compiler_params=limit,
+            cost_estimate=pl.CostEstimate(
+                flops=chunk * 400_000, bytes_accessed=12_000_000, transcendentals=0
+            ),
+        )(chunk_refs, slab)
+
+    def halo_of(density):
+        sides, lower, upper = [], [], []
+        left = SWEEPS
+        hop = 1
+        while left > 0:
+            width = min(planes, left)
+            up = [(order[s], order[s + hop]) for s in range(n_orb - hop)]
+            down = [(j, i) for i, j in up]
+            sides.append(lax.ppermute(density[:, planes - width:], "orb", up))
+            lower = [(len(sides) - 1, k) for k in range(width)] + lower
+            sides.append(lax.ppermute(density[:, :width], "orb", down))
+            upper = upper + [(len(sides) - 1, k) for k in range(width)]
+            left -= width
+            hop += 1
+        return sides, (lower, upper)
+
+    place = jnp.take(seat, me).reshape(1)
+    chunk_refs = [refs[c * chunk:(c + 1) * chunk] for c in range(chunks)]
+    halos = [halo_of(density_of(part)) for part in chunk_refs]
+    field_shape = (n_orbitals, planes, rows, LANES)
+    given = []
+    for c in range(chunks - 1):
+        sides, before = halos[c]
+        given.append(pl.pallas_call(
+            functools.partial(force_kernel, n_orb, before, polynomial(), False),
+            out_shape=jax.ShapeDtypeStruct((chunk, 2, planes, rows, LANES), jnp.float32),
+            in_specs=[smem, smem, vmem] + [vmem] * len(sides),
+            out_specs=vmem,
+            scratch_shapes=[pads(pair_group), pads(pair_group)],
+            compiler_params=limit,
+            cost_estimate=pl.CostEstimate(
+                flops=chunk * 2_000_000, bytes_accessed=20_000_000, transcendentals=0
+            ),
+        )(chunk_refs[c], place, slab, *sides))
+    sides, before = halos[-1]
+    if given:
+        done_refs, done = refs[:(chunks - 1) * chunk], jnp.concatenate(given)
+    else:
+        done_refs, done = refs[:1], jnp.zeros((1, 2, planes, rows, LANES), jnp.float32)
+    rounded = pl.pallas_call(
+        functools.partial(force_kernel, n_orb, before, polynomial(), True),
+        out_shape=jax.ShapeDtypeStruct(field_shape, jnp.bfloat16),
+        in_specs=[smem, smem, vmem] + [vmem] * len(sides) + [smem, vmem],
         out_specs=vmem,
-        scratch_shapes=[pad],
+        scratch_shapes=[pltpu.VMEM(field_shape, jnp.float32), pads(pair_group), pads(pair_group)],
         compiler_params=limit,
-    )(refs, slab)
-
-    sides, lower, upper = [], [], []
-    left = SWEEPS
-    hop = 1
-    while left > 0:
-        width = min(planes, left)
-        up = [(order[s], order[s + hop]) for s in range(n_orb - hop)]
-        down = [(j, i) for i, j in up]
-        sides.append(lax.ppermute(density[:, planes - width:], "orb", up))
-        lower = [(len(sides) - 1, k) for k in range(width)] + lower
-        sides.append(lax.ppermute(density[:, :width], "orb", down))
-        upper = upper + [(len(sides) - 1, k) for k in range(width)]
-        left -= width
-        hop += 1
-
-    rounded = pl.pallas_call(
-        functools.partial(force_kernel, n_orb, (lower, upper), polynomial()),
-        out_shape=jax.ShapeDtypeStruct((n_orbitals, planes, rows, LANES), jnp.bfloat16),
-        in_specs=[smem, smem, vmem] + [vmem] * len(sides),
-        out_specs=vmem,
-        scratch_shapes=[
-            pltpu.VMEM((n_orbitals, planes, rows, LANES), jnp.float32), pad, pad,
-        ],
-        compiler_params=limit,
-    )(refs, jnp.take(seat, me).reshape(1), slab, *sides)
+    )(chunk_refs[-1], place, slab, *sides, done_refs, done)
 
     returned = exchange(rounded.reshape(n_orb, orb_dev, planes, rows, LANES))
-    exch_force = returned.astype(jnp.float32).transpose(1, 0, 2, 3, 4)
-    exch_force = exch_force.reshape(orb_dev, box_planes, flat_cells)
+    exch_force = pl.pallas_call(
+        collect_kernel,
+        grid=(orb_dev,),
+        out_shape=jax.ShapeDtypeStruct((orb_dev, box_planes, flat_cells), jnp.float32),
+        in_specs=[pl.BlockSpec((n_orb, 1, planes, rows, LANES), lambda k: (0, k, 0, 0, 0))],
+        out_specs=pl.BlockSpec((1, box_planes, flat_cells), lambda k: (k, 0, 0)),
+        scratch_shapes=[pltpu.VMEM((box_planes * rows, LANES), jnp.float32)],
+    )(returned)
 
     intersection = lax.dot_general(
         slab.reshape(n_orbitals, -1), rounded.reshape(n_orbitals, -1),
@@ -347,11 +463,13 @@
     blocks = blocks.reshape(n_orb * n_orb, orb_dev * orb_dev)
     chosen = jnp.take(seat, tiles[:, 0]) * n_orb + jnp.take(seat, tiles[:, 1])
     picked = jnp.take(blocks, chosen, axis=0).reshape(n_orb, -1)
-    parts = jnp.concatenate([jnp.take(picked, np.asarray(order), axis=0), self_part], axis=1)
-    summed = jnp.sum(exchange(parts), axis=0)
+    parts = jnp.concatenate([picked, jnp.take(self_part, np.asarray(position), axis=0)], axis=1)
     width = picked.shape[1]
+    spare = -parts.shape[1] % (8 * LANES)
+    parts = jnp.pad(parts, ((0, 0), (0, spare))).reshape(n_orb, -1, LANES)
+    summed = reduce_parts(parts, n_orb, me).reshape(-1)
     tile_rows = summed[:width].reshape(-1, orb_dev * orb_dev)
-    return exch_force, tile_rows * BOX ** (-1.5), summed[width:] * BOX ** (-2.5)
+    return exch_force, tile_rows * BOX ** (-1.5), summed[width:width + orb_dev] * BOX ** (-2.5)
 
 
 def body(orbitals, pairs, tiles):

time: 649 us -> 563 us (0.87)
  waiting for transfers between devices: 396 us -> 346 us
  local copies, waits for them, and re-layouts: 95.5 us -> 46.7 us
  Pallas kernels: 89.2 us -> 112 us
  other arithmetic: 14 us -> 2.15 us
  starting transfers between devices: 25.6 us -> 37.2 us
  blocking collectives: 11 us -> 0 us
    all_to_all x1, waiting for transfers between devices: 187 us -> 0.01 us  [slab_body(): returned = exchange(rounded.reshape(n_orb, orb_dev, planes, rows, LANES))]
    ppermute x4 -> x13, waiting for transfers between devices: 24 us -> 161 us  [the longest x5 149 us: reduce_parts(): lax.ppermute(sent, 'orb', [(d, d ^ bit) for d in range(n_orb)])]
    reshape x3 -> x0, local copies, waits for them, and re-layouts: 40.1 us -> none  [the longest x2 30.5 us: slab_body(): exch_force = exch_force.reshape(orb_dev, box_planes, flat_cells)]
    pallas_call x2 -> x6, Pallas kernels: 89.2 us -> 112 us  [the longest x2 60.7 us: slab_body(): pl.pallas_call(functools.partial(force_kernel, n_orb, before, polynomial(...]
    reshape x1 -> x0, other arithmetic: 11.9 us -> none  [slab_body(): exch_force = exch_force.reshape(orb_dev, box_planes, flat_cells)]
    all_to_all x1 -> x0, blocking collectives: 11 us -> none  [slab_body(): summed = jnp.sum(exchange(parts), axis=0)]
    unnamed x11 -> x16, local copies, waits for them, and re-layouts: 10.9 us -> 1.99 us
    ppermute x4 -> x13, starting transfers between devices: 8.42 us -> 17.1 us  [the longest x4 9.15 us: halo_of(): sides.append(lax.ppermute(density[:, planes - width:], 'orb', up))]
  transfers between devices with their start and end apart: 7 -> 16, of which waited for: 4 -> 7; matrix products, arithmetic and copies ran while one was open for 6% -> 11% of each run, Pallas kernels for 0% -> 9%
where the time goes in v2:
time: 563 us; the launch traced here: 561 us
  waiting for transfers between devices  346 us (61%)
  Pallas kernels  112 us (20%)
  local copies, waits for them, and re-layouts  46.7 us (8%)
  starting transfers between devices  37.2 us (7%)
  matrix products  14.8 us (3%)
    all_to_all x1, waiting for transfers between devices, slab_body(): slab = exchange(leaving).reshape(n_orbitals, planes, rows, LANES)  185 us
    ppermute x5, waiting for transfers between devices, reduce_parts(): lax.ppermute(sent, 'orb', [(d, d ^ bit) for d in range(n_orb)])  149 us
    pallas_call x2, Pallas kernels, slab_body(): pl.pallas_call(functools.partial(force_kernel, n_orb, before, polynomial(...  60.7 us
    pallas_call x1, Pallas kernels, slab_body(): pl.pallas_call(spread_kernel, grid=(orb_dev,), out_shape=jax.ShapeDtypeSt...  20.5 us
    pallas_call x1, Pallas kernels, slab_body(): pl.pallas_call(collect_kernel, grid=(orb_dev,), out_shape=jax.ShapeDtypeS...  18.3 us
    dot_general x1, matrix products, slab_body(): lax.dot_general(slab.reshape(n_orbitals, -1), rounded.reshape(n_orbitals,...  14.8 us
    another operation x1, local copies, waits for them, and re-layouts, slab_body(): slab.reshape(n_orbitals, -1)  13.4 us
    pallas_call x2, Pallas kernels, density_of(): pl.pallas_call(density_kernel, out_shape=jax.ShapeDtypeStruct((chunk, pla...  12.7 us
  transfers between devices with their start and end apart: 16, of which 7 were waited for; matrix products, arithmetic and copies ran while one was open for 11% of the time, Pallas kernels for 9%

profile of v2, /device:TPU:0, one launch (start us, length us, event | category | flops | bytes accessed | tf_op | source)
XLA Modules:
  0.0 561.2 jit_solution(2394298805919775558)
XLA Ops:
  0.6 1.3 broadcast_in_dim.52
  1.9 7.3 %all-to-all-start = ((s32[32,4,4]{2,1,0:T(4,128)}), s32[32,4,4]{2,1,0:T(4,128)S(1)}, u32[]{:S(2)}, u32[]{:S(2)}) async-start(s32[32,4,4]{2,1,0:T(4,128)} %broadcast_in_dim.52), calls=%async_computation | async-start | bytes 131072 | tf_op jit(solution)/shard_map/all_to_all | solution.py:369
  9.3 20.5 %shard_map.76 = bf16[32,16,2,32,128]{4,3,2,1,0:T(8,128)(2,1)} custom-call(bf16[16,64,4096]{2,1,0:T(8,128)(2,1)} %own.1), custom_call_target="tpu_custom_call" | custom-call | tf_op jit(solution)/shard_map/pallas_call | solution.py:360
  29.7 6.0 %all-to-all-start.1 = ((bf16[32,16,2,32,128]{4,3,2,1,0:T(8,128)(2,1)}), bf16[32,16,2,32,128]{4,3,2,1,0:T(8,128)(2,1)}, u32[]{:S(2)}, u32[]{:S(2)}) async-start(bf16[32,16,2,32,128]{4,3,2,1,0:T(8,128)(2,1)} %shard_map.76), calls=%async_computation.1 | async-start | bytes 16777216 | tf_op jit(solution)/shard_map/all_to_all | solution.py:368
  35.9 1.9 gather_fusion
  38.8 185.2 %all-to-all-done.1 = bf16[32,16,2,32,128]{4,3,2,1,0:T(8,128)(2,1)} async-done(((bf16[32,16,2,32,128]{4,3,2,1,0:T(8,128)(2,1)}), bf16[32,16,2,32,128]{4,3,2,1,0:T(8,128)(2,1)}, u32[]{:S(2)}, u32[]{:S(2)}) %all-to-all-start.1) | async-done | bytes 8388640 | tf_op jit(solution)/shard_map/all_to_all | solution.py:368
  223.9 6.4 %shard_map.78 = bf16[64,2,32,128]{3,2,1,0:T(8,128)(2,1)} custom-call(s32[64,4]{1,0:T(8,128)} %get-tuple-element.34.refs.rest_4_, bf16[512,2,32,128]{3,2,1,0:T(8,128)(2,1)} %bitcast.2.slab), custom_call_target="tpu_custom_call" | custom-call | flops 25600000 | bytes 12000000 | tf_op jit(solution)/shard_map/pallas_call | solution.py:387
  230.3 1.5 collective-permute-start.4
  233.1 1.3 collective-permute-start.6
  234.5 1.3 collective-permute-start.5
  235.8 1.3 collective-permute-start.7
  237.1 6.3 %shard_map.77 = bf16[64,2,32,128]{3,2,1,0:T(8,128)(2,1)} custom-call(s32[64,4]{1,0:T(8,128)} %get-tuple-element.35.refs, bf16[512,2,32,128]{3,2,1,0:T(8,128)(2,1)} %bitcast.2.slab), custom_call_target="tpu_custom_call" | custom-call | flops 25600000 | bytes 12000000 | tf_op jit(solution)/shard_map/pallas_call | solution.py:387
  243.4 3.3 collective-permute-start
  246.8 1.3 collective-permute-start.1
  248.1 2.3 fusion.12
  250.3 12.6 %collective-permute-done.7.rest_3_ = bf16[64,1,32,128]{3,2,1,0:T(8,128)(2,1)S(1)} collective-permute-done((bf16[64,1,32,128]{3,2,1,0:T(8,128)(2,1)S(1)}, bf16[64,1,32,128]{3,2,1,0:T(8,128)(2,1)S(1)}, u32[]{:S(2)}, u32[]{:S(2)}) %collective-permute-start.7) | collective-permute-done | bytes 524320 | tf_op jit(solution)/shard_map/ppermute | solution.py:409
  263.0 3.0 collective-permute-start.2
  269.5 25.3 %shard_map.79.rest_5_ = f32[64,2,2,32,128]{4,3,2,1,0:T(8,128)} custom-call(s32[64,4]{1,0:T(8,128)} %get-tuple-element.34.refs.rest_4_, s32[1]{0:T(128)S(6)} %select_n.151.place, bf16[512,2,32,128]{3,2,1,0:T(8,128)(2,1)} %bitcast.2.slab, bf16[64,2,32,128]{3,2,1,0:T(8,128)(2,1)} %copy-done.1, bf16[64,2,32,128]{3,2,1,0:T(8,128)(2,1)} %copy-done.2, ...), custom_call_target="tpu_custom_call" | custom-call | flops 128000000 | bytes 20000000 | tf_op jit(solution)/shard_map/pallas_call | solution.py:422
  295.8 35.5 %shard_map.80 = bf16[512,2,32,128]{3,2,1,0:T(8,128)(2,1)} custom-call(s32[64,4]{1,0:T(8,128)} %get-tuple-element.35.refs, s32[1]{0:T(128)S(6)} %select_n.151.place, bf16[512,2,32,128]{3,2,1,0:T(8,128)(2,1)} %bitcast.2.slab, bf16[64,2,32,128]{3,2,1,0:T(8,128)(2,1)} %copy-done.3, bf16[64,2,32,128]{3,2,1,0:T(8,128)(2,1)} %collective-permute-done.1.rest_1_, ...), custom_call_target="tpu_custom_call" | custom-call | tf_op jit(solution)/shard_map/pallas_call | solution.py:438
  331.2 6.8 %all-to-all-start.2 = ((bf16[32,16,2,32,128]{4,3,2,1,0:T(8,128)(2,1)}), bf16[32,16,2,32,128]{4,3,2,1,0:T(8,128)(2,1)}, u32[]{:S(2)}, u32[]{:S(2)}) async-start(bf16[32,16,2,32,128]{4,3,2,1,0:T(8,128)(2,1)} %bitcast.43), calls=%async_computation.2 | async-start | bytes 16777216 | tf_op jit(solution)/shard_map/all_to_all | solution.py:447
  339.6 13.4 %reshape_reshape.3 = bf16[512,8192]{1,0:T(8,128)(2,1)} reshape(bf16[32,16,2,32,128]{4,3,2,1,0:T(8,128)(2,1)} %all-to-all-done.1) | data formatting | bytes 16777216 | tf_op jit(solution)/shard_map/reshape;reshape | solution.py:458
  352.9 14.8 %fusion.3 = f32[512,512]{0,1:T(8,128)S(1)} fusion(bf16[512,8192]{1,0:T(8,128)(2,1)} %reshape_reshape.3, bf16[64,8,64,128]{3,2,1,0:T(8,128)(2,1)} %bitcast.44), kind=kOutput, calls=%fused_computation.9 | convolution fusion | flops 4294967296 | bytes 17825792 | tf_op jit(solution)/shard_map/dot_general | solution.py:457
  368.1 4.9 reshape.84
  373.0 7.2 %copy.21 = f32[32,32,16,16]{1,0,3,2:T(8,128)} copy(f32[32,32,16,16]{3,1,2,0:T(8,128)} %bitcast.42) | data formatting | bytes 2097152 | tf_op jit(solution)/shard_map/transpose | solution.py:462
  380.2 3.7 reshape.85
  384.3 4.5 gather_fusion.2
  390.3 2.5 collective-permute-start.8
  392.8 136.2 %collective-permute-done.8 = f32[16,8,128]{2,1,0:T(8,128)S(1)} collective-permute-done((f32[16,8,128]{2,1,0:T(8,128)S(1)}, f32[16,8,128]{2,1,0:T(8,128)S(1)}, u32[]{:S(2)}, u32[]{:S(2)}) %collective-permute-start.8) | collective-permute-done | bytes 65568 | tf_op jit(solution)/shard_map/ppermute | solution.py:339
  529.1 3.9 collective-permute-done.9
  533.1 3.7 collective-permute-done.10
  536.9 3.6 collective-permute-done.11
  542.8 18.3 %shard_map.81 = f32[16,64,4096]{2,1,0:T(8,128)} custom-call(bf16[32,16,2,32,128]{4,3,2,1,0:T(8,128)(2,1)} %all-to-all-done.2.back), custom_call_target="tpu_custom_call" | custom-call | tf_op jit(solution)/shard_map/pallas_call | solution.py:448
  (66 shorter events, 12.4 us)
Async XLA Ops:
  1.9 27.8 %all-to-all-start = ((s32[32,4,4]{2,1,0:T(4,128)}), s32[32,4,4]{2,1,0:T(4,128)S(1)}, u32[]{:S(2)}, u32[]{:S(2)}) async-start(s32[32,4,4]{2,1,0:T(4,128)} %broadcast_in_dim.52), calls=%async_computation | async-start | bytes 131072 | tf_op jit(solution)/shard_map/all_to_all | solution.py:369
  29.7 6.2 %copy-start = (s32[32]{0:T(128)S(1)}, s32[32]{0:T(128)}, u32[]{:S(2)}) copy-start(s32[32]{0:T(128)} %constant.120.clone) | copy-start | bytes 388
  29.7 194.2 %all-to-all-start.1 = ((bf16[32,16,2,32,128]{4,3,2,1,0:T(8,128)(2,1)}), bf16[32,16,2,32,128]{4,3,2,1,0:T(8,128)(2,1)}, u32[]{:S(2)}, u32[]{:S(2)}) async-start(bf16[32,16,2,32,128]{4,3,2,1,0:T(8,128)(2,1)} %shard_map.76), calls=%async_computation.1 | async-start | bytes 16777216 | tf_op jit(solution)/shard_map/all_to_all | solution.py:368
  230.3 35.6 %collective-permute-start.4 = (bf16[64,2,32,128]{3,2,1,0:T(8,128)(2,1)}, bf16[64,2,32,128]{3,2,1,0:T(8,128)(2,1)S(1)}, u32[]{:S(2)}, u32[]{:S(2)}) collective-permute-start(bf16[64,2,32,128]{3,2,1,0:T(8,128)(2,1)} %shard_map.78), channel_id=1, source_target_pairs={{0,1},{1,2},{2,3},{3,6},{6,7},{7,4},{4,5},{5,12},{12,13},{13,14},{... | collective-permute-start | bytes 3145736 | tf_op jit(solution)/shard_map/ppermute | solution.py:407
  233.1 13.6 %collective-permute-start.6 = (bf16[64,1,32,128]{3,2,1,0:T(8,128)(2,1)S(1)}, bf16[64,1,32,128]{3,2,1,0:T(8,128)(2,1)S(1)}, u32[]{:S(2)}, u32[]{:S(2)}) collective-permute-start(bf16[64,1,32,128]{3,2,1,0:T(8,128)(2,1)S(1)} %get-tuple-element.29), channel_id=1, source_target_pairs={{0,2},{1,3},{2,6},{3,7},{6,4},{7,5},{4,12},{5,13},{12,14},{13,15},... | collective-permute-start | bytes 1572872 | tf_op jit(solution)/shard_map/ppermute | solution.py:407
  234.5 34.1 %collective-permute-start.5 = (bf16[64,2,32,128]{3,2,1,0:T(8,128)(2,1)}, bf16[64,2,32,128]{3,2,1,0:T(8,128)(2,1)S(1)}, u32[]{:S(2)}, u32[]{:S(2)}) collective-permute-start(bf16[64,2,32,128]{3,2,1,0:T(8,128)(2,1)} %shard_map.78), channel_id=1, source_target_pairs={{1,0},{2,1},{3,2},{6,3},{7,6},{4,7},{5,4},{12,5},{13,12},{14,13},{... | collective-permute-start | bytes 3145736 | tf_op jit(solution)/shard_map/ppermute | solution.py:409
  235.8 27.2 %collective-permute-start.7 = (bf16[64,1,32,128]{3,2,1,0:T(8,128)(2,1)S(1)}, bf16[64,1,32,128]{3,2,1,0:T(8,128)(2,1)S(1)}, u32[]{:S(2)}, u32[]{:S(2)}) collective-permute-start(bf16[64,1,32,128]{3,2,1,0:T(8,128)(2,1)S(1)} %get-tuple-element.28), channel_id=1, source_target_pairs={{2,0},{3,1},{6,2},{7,3},{4,6},{5,7},{12,4},{13,5},{14,12},{15,13},... | collective-permute-start | bytes 1572872 | tf_op jit(solution)/shard_map/ppermute | solution.py:409
  243.4 51.4 %collective-permute-start = (bf16[64,2,32,128]{3,2,1,0:T(8,128)(2,1)}, bf16[64,2,32,128]{3,2,1,0:T(8,128)(2,1)S(1)}, u32[]{:S(2)}, u32[]{:S(2)}) collective-permute-start(bf16[64,2,32,128]{3,2,1,0:T(8,128)(2,1)} %shard_map.77), channel_id=1, source_target_pairs={{0,1},{1,2},{2,3},{3,6},{6,7},{7,4},{4,5},{5,12},{12,13},{13,14},{... | collective-permute-start | bytes 3145736 | tf_op jit(solution)/shard_map/ppermute | solution.py:407
  246.7 19.2 %copy-start.4 = (bf16[64,1,32,128]{3,2,1,0:T(8,128)(2,1)}, bf16[64,1,32,128]{3,2,1,0:T(8,128)(2,1)S(1)}, u32[]{:S(2)}) copy-start(bf16[64,1,32,128]{3,2,1,0:T(8,128)(2,1)S(1)} %collective-permute-done.6.rest_2_) | copy-start | bytes 1572868
  246.8 48.0 %collective-permute-start.1 = (bf16[64,2,32,128]{3,2,1,0:T(8,128)(2,1)}, bf16[64,2,32,128]{3,2,1,0:T(8,128)(2,1)}, u32[]{:S(2)}, u32[]{:S(2)}) collective-permute-start(bf16[64,2,32,128]{3,2,1,0:T(8,128)(2,1)} %shard_map.77), channel_id=1, source_target_pairs={{1,0},{2,1},{3,2},{6,3},{7,6},{4,7},{5,4},{12,5},{13,12},{14,13},{... | collective-permute-start | bytes 3145736 | tf_op jit(solution)/shard_map/ppermute | solution.py:409
  263.0 3.0 copy-start.5
  263.0 31.8 %collective-permute-start.2 = (bf16[64,1,32,128]{3,2,1,0:T(8,128)(2,1)}, bf16[64,1,32,128]{3,2,1,0:T(8,128)(2,1)}, u32[]{:S(2)}, u32[]{:S(2)}) collective-permute-start(bf16[64,1,32,128]{3,2,1,0:T(8,128)(2,1)} %get-tuple-element.31), channel_id=1, source_target_pairs={{0,2},{1,3},{2,6},{3,7},{6,4},{7,5},{4,12},{5,13},{12,14},{13,15},... | collective-permute-start | bytes 1572872 | tf_op jit(solution)/shard_map/ppermute | solution.py:407
  266.0 2.6 copy-start.1
  266.0 28.8 %collective-permute-start.3 = (bf16[64,1,32,128]{3,2,1,0:T(8,128)(2,1)}, bf16[64,1,32,128]{3,2,1,0:T(8,128)(2,1)}, u32[]{:S(2)}, u32[]{:S(2)}) collective-permute-start(bf16[64,1,32,128]{3,2,1,0:T(8,128)(2,1)} %get-tuple-element.30), channel_id=1, source_target_pairs={{2,0},{3,1},{6,2},{7,3},{4,6},{5,7},{12,4},{13,5},{14,12},{15,13},... | collective-permute-start | bytes 1572872 | tf_op jit(solution)/shard_map/ppermute | solution.py:409
  268.5 1.0 copy-start.2
  294.8 1.0 copy-start.3
  331.2 6.8 %copy-start.6 = (s32[32,2]{0,1:T(2,128)S(1)}, s32[32,2]{0,1:T(2,128)}, u32[]{:S(2)}) copy-start(s32[32,2]{0,1:T(2,128)} %param.9) | copy-start | bytes 772
  331.2 211.6 %all-to-all-start.2 = ((bf16[32,16,2,32,128]{4,3,2,1,0:T(8,128)(2,1)}), bf16[32,16,2,32,128]{4,3,2,1,0:T(8,128)(2,1)}, u32[]{:S(2)}, u32[]{:S(2)}) async-start(bf16[32,16,2,32,128]{4,3,2,1,0:T(8,128)(2,1)} %bitcast.43), calls=%async_computation.2 | async-start | bytes 16777216 | tf_op jit(solution)/shard_map/all_to_all | solution.py:447
  390.3 138.7 %collective-permute-start.8 = (f32[16,8,128]{2,1,0:T(8,128)S(1)}, f32[16,8,128]{2,1,0:T(8,128)S(1)}, u32[]{:S(2)}, u32[]{:S(2)}) collective-permute-start(f32[16,8,128]{2,1,0:T(8,128)S(1)} %bitcast.47), channel_id=1, source_target_pairs={{0,16},{1,17},{2,18},{3,19},{4,20},{5,21},{6,22},{7,23},{8,24},{9,... | collective-permute-start | bytes 196616 | tf_op jit(solution)/shard_map/ppermute | solution.py:339
  529.0 4.0 collective-permute-start.9
  533.0 3.8 collective-permute-start.10
  536.8 3.7 collective-permute-start.11
  540.5 1.2 collective-permute-start.12

commit v3 on v2

--- a/solution.py
+++ b/solution.py
@@ -211,7 +211,7 @@
     lax.fori_loop(0, out.shape[0] // width, group, 0)
 
 
-def spread_kernel(own, out, lines):
+def spread_kernel(chosen, own, out, lines):
     box_planes, flat_cells = own.shape[1:]
     slabs, _, planes, rows, lanes = out.shape
     for r in range(rows):
@@ -221,10 +221,16 @@
     out[...] = lines[...].reshape(out.shape).astype(out.dtype)
 
 
-def collect_kernel(back, out, lines):
+def orb_count(slots):
+    return slots.shape[0] // 2
+
+
+def collect_kernel(slots, back, out, lines):
     box_planes, flat_cells = out.shape[1:]
     slabs, _, planes, rows, lanes = back.shape
-    lines[...] = back[...].astype(jnp.float32).reshape(lines.shape)
+    named = slots[orb_count(slots) + pl.program_id(0)] > 0
+    values = back[...].astype(jnp.float32).reshape(lines.shape)
+    lines[...] = jnp.where(named, values, 0.0)
     for r in range(rows):
         out[0, :, r * lanes:(r + 1) * lanes] = lines[pl.ds(r, box_planes, stride=rows), :]
 
@@ -330,55 +336,93 @@
         return jnp.sum(
             lax.all_to_all(parts, "orb", split_axis=0, concat_axis=0, tiled=True), axis=0
         )
-    bit = n_orb // 2
-    while bit:
+    bit = 1
+    while bit < n_orb:
         upper = (me & bit) != 0
-        low, high = parts[:bit], parts[bit:]
+        halves = parts.reshape((-1, 2) + parts.shape[1:])
+        low, high = halves[:, 0], halves[:, 1]
         sent = jnp.where(upper, low, high)
         kept = jnp.where(upper, high, low)
         parts = kept + lax.ppermute(sent, "orb", [(d, d ^ bit) for d in range(n_orb)])
-        bit //= 2
+        bit *= 2
     return parts
 
 
 def slab_body(orbitals, pairs, tiles):
+    n_orb = lax.axis_size("orb")
+    orb_dev = orbitals.shape[0]
+    order = chain(n_orb)
+    position = [order.index(d) for d in range(n_orb)]
+    exchange = functools.partial(
+        lax.all_to_all, axis_name="orb", split_axis=0, concat_axis=0, tiled=True,
+        axis_index_groups=[order],
+    )
+    seat = jnp.asarray(position, jnp.int32)
+    me = lax.axis_index("orb")
+    every = exchange(jnp.broadcast_to(pairs[None], (n_orb,) + pairs.shape)).reshape(-1, 4)
+
+    ids = every[:, :2].reshape(-1)
+    kinds = jnp.arange(n_orb * orb_dev, dtype=jnp.int32)
+    named = jnp.any(ids[:, None] == kinds[None, :], axis=0).reshape(n_orb, orb_dev)
+    locals_ = jnp.arange(orb_dev, dtype=jnp.int32)
+    earlier = locals_[None, :] < locals_[:, None]
+    before = jnp.sum((named[:, None, :] & earlier[None]).astype(jnp.int32), axis=2)
+    total = jnp.sum(named.astype(jnp.int32), axis=1, keepdims=True)
+    slots = jnp.where(named, before, total + locals_[None, :] - before)
+    own_slots = lax.dynamic_index_in_dim(slots, me, 0, keepdims=False)
+    chosen = jnp.sum(
+        jnp.where(own_slots[None, :] == locals_[:, None], locals_[None, :], 0), axis=1
+    ).astype(jnp.int32)
+
+    def plan(capacity):
+        return functools.partial(slab_plan, capacity, order, position, exchange)
+
+    operands = (orbitals, every, tiles, slots, own_slots, chosen)
+    capacity = orb_dev * 3 // 4
+    return lax.cond(jnp.max(total) <= capacity, plan(capacity), plan(orb_dev), *operands)
+
+
+def slab_plan(capacity, order, position, exchange, orbitals, every, tiles, slots, own_slots, chosen):
     n_orb = lax.axis_size("orb")
     orb_dev, box_planes, flat_cells = orbitals.shape
     planes = box_planes // n_orb
     rows = flat_cells // LANES
-    n_orbitals = n_orb * orb_dev
-    order = chain(n_orb)
-    position = [order.index(d) for d in range(n_orb)]
-    groups = [order]
-    exchange = functools.partial(
-        lax.all_to_all, axis_name="orb", split_axis=0, concat_axis=0, tiled=True,
-        axis_index_groups=groups,
-    )
     seat = jnp.asarray(position, jnp.int32)
     me = lax.axis_index("orb")
-
-    leaving = pl.pallas_call(
-        spread_kernel,
-        grid=(orb_dev,),
-        out_shape=jax.ShapeDtypeStruct((n_orb, orb_dev, planes, rows, LANES), orbitals.dtype),
-        in_specs=[pl.BlockSpec((1, box_planes, flat_cells), lambda k: (k, 0, 0))],
-        out_specs=pl.BlockSpec((n_orb, 1, planes, rows, LANES), lambda k: (0, k, 0, 0, 0)),
-        scratch_shapes=[pltpu.VMEM((box_planes * rows, LANES), jnp.float32)],
-    )(orbitals)
-    slab = exchange(leaving).reshape(n_orbitals, planes, rows, LANES)
-    every = exchange(jnp.broadcast_to(pairs[None], (n_orb,) + pairs.shape)).reshape(-1, 4)
+    lines = pltpu.VMEM((box_planes * rows, LANES), jnp.float32)
+
+    def leaving(first, count):
+        return pl.pallas_call(
+            spread_kernel,
+            grid_spec=pltpu.PrefetchScalarGridSpec(
+                num_scalar_prefetch=1,
+                grid=(count,),
+                in_specs=[
+                    pl.BlockSpec((1, box_planes, flat_cells), lambda k, c: (c[first + k], 0, 0))
+                ],
+                out_specs=pl.BlockSpec(
+                    (n_orb, 1, planes, rows, LANES), lambda k, c: (0, k, 0, 0, 0)
+                ),
+                scratch_shapes=[lines],
+            ),
+            out_shape=jax.ShapeDtypeStruct((n_orb, count, planes, rows, LANES), orbitals.dtype),
+        )(chosen, orbitals)
+
+    slab = exchange(leaving(0, capacity)).reshape(n_orb * capacity, planes, rows, LANES)
     ids = every[:, :2]
-    slots = jnp.take(seat, ids // orb_dev) * orb_dev + ids % orb_dev
-    refs = jnp.concatenate([slots, every[:, 2:]], axis=1)
+    owners = ids // orb_dev
+    at = jnp.take(seat, owners) * capacity + jnp.take(slots.reshape(-1), ids)
+    refs = jnp.concatenate([at, every[:, 2:]], axis=1)
     n_pairs = refs.shape[0]
 
     vmem = pl.BlockSpec(memory_space=pltpu.VMEM)
     smem = pl.BlockSpec(memory_space=pltpu.SMEM)
     limit = pltpu.CompilerParams(vmem_limit_bytes=58 * 1024 * 1024)
-    chunks = 2 if n_pairs % 8 == 0 else 1
+    fast = capacity < orb_dev
+    chunks = 2 if fast and n_pairs % 8 == 0 else 1
     chunk = n_pairs // chunks
-    group = math.gcd(chunk, 4)
-    pair_group = math.gcd(chunk, 2)
+    group = math.gcd(chunk, 4) if fast else 1
+    pair_group = math.gcd(chunk, 2) if fast else 1
 
     def pads(count):
         return pltpu.VMEM((count, planes, rows + 2 * PAD, LANES), jnp.float32)
@@ -415,7 +459,8 @@
     place = jnp.take(seat, me).reshape(1)
     chunk_refs = [refs[c * chunk:(c + 1) * chunk] for c in range(chunks)]
     halos = [halo_of(density_of(part)) for part in chunk_refs]
-    field_shape = (n_orbitals, planes, rows, LANES)
+
+    field_shape = (n_orb * capacity, planes, rows, LANES)
     given = []
     for c in range(chunks - 1):
         sides, before = halos[c]
@@ -431,6 +476,12 @@
             ),
         )(chunk_refs[c], place, slab, *sides))
     sides, before = halos[-1]
+    rest = None
+    if fast:
+        later = leaving(capacity, orb_dev - capacity)
+        ready = given or sides
+        rest = exchange(lax.optimization_barrier([later] + ready)[0])
+        rest = rest.reshape(n_orb * (orb_dev - capacity), -1)
     if given:
         done_refs, done = refs[:(chunks - 1) * chunk], jnp.concatenate(given)
     else:
@@ -442,28 +493,65 @@
         out_specs=vmem,
         scratch_shapes=[pltpu.VMEM(field_shape, jnp.float32), pads(pair_group), pads(pair_group)],
         compiler_params=limit,
+        cost_estimate=pl.CostEstimate(
+            flops=chunk * 3_000_000, bytes_accessed=30_000_000, transcendentals=0
+        ),
     )(chunk_refs[-1], place, slab, *sides, done_refs, done)
 
-    returned = exchange(rounded.reshape(n_orb, orb_dev, planes, rows, LANES))
+    returned = exchange(rounded.reshape(n_orb, capacity, planes, rows, LANES))
+    own_named = (own_slots < capacity).astype(jnp.int32)
+    source = jnp.concatenate([jnp.minimum(own_slots, capacity - 1), own_named])
     exch_force = pl.pallas_call(
         collect_kernel,
-        grid=(orb_dev,),
+        grid_spec=pltpu.PrefetchScalarGridSpec(
+            num_scalar_prefetch=1,
+            grid=(orb_dev,),
+            in_specs=[
+                pl.BlockSpec(
+                    (n_orb, 1, planes, rows, LANES), lambda k, c: (0, c[k], 0, 0, 0)
+                )
+            ],
+            out_specs=pl.BlockSpec((1, box_planes, flat_cells), lambda k, c: (k, 0, 0)),
+            scratch_shapes=[lines],
+        ),
         out_shape=jax.ShapeDtypeStruct((orb_dev, box_planes, flat_cells), jnp.float32),
-        in_specs=[pl.BlockSpec((n_orb, 1, planes, rows, LANES), lambda k: (0, k, 0, 0, 0))],
-        out_specs=pl.BlockSpec((1, box_planes, flat_cells), lambda k: (k, 0, 0)),
-        scratch_shapes=[pltpu.VMEM((box_planes * rows, LANES), jnp.float32)],
-    )(returned)
-
-    intersection = lax.dot_general(
-        slab.reshape(n_orbitals, -1), rounded.reshape(n_orbitals, -1),
-        (((1,), (1,)), ((), ())), preferred_element_type=jnp.float32,
-    )
-    self_part = jnp.diagonal(intersection).reshape(n_orb, orb_dev)
-    blocks = intersection.reshape(n_orb, orb_dev, n_orb, orb_dev).transpose(0, 2, 1, 3)
-    blocks = blocks.reshape(n_orb * n_orb, orb_dev * orb_dev)
-    chosen = jnp.take(seat, tiles[:, 0]) * n_orb + jnp.take(seat, tiles[:, 1])
-    picked = jnp.take(blocks, chosen, axis=0).reshape(n_orb, -1)
-    parts = jnp.concatenate([picked, jnp.take(self_part, np.asarray(position), axis=0)], axis=1)
+        cost_estimate=pl.CostEstimate(
+            flops=4_000_000, bytes_accessed=60_000_000, transcendentals=0
+        ),
+    )(source, returned)
+
+    def against(left):
+        return lax.dot_general(
+            left, rounded.reshape(n_orb * capacity, -1), (((1,), (1,)), ((), ())),
+            preferred_element_type=jnp.float32,
+        ).reshape(n_orb, -1, n_orb, capacity)
+
+    blocks = against(slab.reshape(n_orb * capacity, -1))
+    ranks = jnp.arange(capacity, dtype=jnp.int32)
+    own_part = jnp.sum(
+        jnp.where(jnp.eye(n_orb, dtype=bool)[:, None, :, None]
+                  & jnp.eye(capacity, dtype=bool)[None, :, None, :], blocks, 0.0), axis=(2, 3)
+    )
+    if rest is not None:
+        blocks = jnp.concatenate([blocks, against(rest)], axis=1)
+    blocks = blocks.transpose(0, 2, 1, 3).reshape(n_orb * n_orb, orb_dev * capacity)
+    chosen_blocks = jnp.take(seat, tiles[:, 0]) * n_orb + jnp.take(seat, tiles[:, 1])
+    picked = jnp.take(blocks, chosen_blocks, axis=0).reshape(-1, orb_dev, capacity)
+    row_slots = jnp.take(slots, tiles[:, 0], axis=0)
+    column_slots = jnp.take(slots, tiles[:, 1], axis=0)
+    places = jnp.arange(orb_dev, dtype=jnp.int32)
+    picked = jnp.sum(
+        jnp.where((row_slots[:, :, None] == places)[..., None], picked[:, None], 0.0), axis=2
+    )
+    picked = jnp.sum(
+        jnp.where((column_slots[:, :, None] == ranks)[:, None], picked[:, :, None, :], 0.0), axis=3
+    )
+    picked = picked.reshape(n_orb, -1)
+    own_part = jnp.take(own_part, np.asarray(position), axis=0)
+    self_part = jnp.sum(
+        jnp.where(slots[:, :, None] == ranks, own_part[:, None, :], 0.0), axis=2
+    )
+    parts = jnp.concatenate([picked, self_part], axis=1)
     width = picked.shape[1]
     spare = -parts.shape[1] % (8 * LANES)
     parts = jnp.pad(parts, ((0, 0), (0, spare))).reshape(n_orb, -1, LANES)

time: 563 us -> 527 us (0.936)
  waiting for transfers between devices: 346 us -> 238 us
  starting transfers between devices: 37.2 us -> 73.3 us
  matrix products: 14.8 us -> 29.3 us
  local copies, waits for them, and re-layouts: 46.7 us -> 55.1 us
  loops' own time: 0 us -> 6.16 us
    ppermute x5, waiting for transfers between devices: 149 us -> 55.9 us  [reduce_parts(): lax.ppermute(sent, 'orb', [(d, d ^ bit) for d in range(n_orb)])]
    all_to_all x2 -> x3, waiting for transfers between devices: 185 us -> 134 us  [the longest x1 134 us: slab_plan(): exchange(leaving(0, capacity))]
    dot_general x1 -> x3, local copies, waits for them, and re-layouts: 0.33 us -> 23.5 us  [against(): lax.dot_general(left, rounded.reshape(n_orb * capacity, -1), (((1,), (1,)...]
    all_to_all x2 -> x3, starting transfers between devices: 12.8 us -> 35.5 us  [the longest x1 25.8 us: slab_plan(): returned = exchange(rounded.reshape(n_orb, capacity, planes, rows, LANES))]
    ppermute x4, waiting for transfers between devices: 0.01 us -> 17.2 us  [halo_of(): sides.append(lax.ppermute(density[:, planes - width:], 'orb', up))]
    dot_general x1 -> x2, matrix products: 14.8 us -> 29.3 us  [against(): lax.dot_general(left, rounded.reshape(n_orb * capacity, -1), (((1,), (1,)...]
    another operation x2 -> x1, local copies, waits for them, and re-layouts: 13.9 us -> 0.07 us  [the longest x1 13.4 us: slab_body(): slab.reshape(n_orbitals, -1)]
    ppermute x4, waiting for transfers between devices: 12.6 us -> 24.2 us  [halo_of(): sides.append(lax.ppermute(density[:, :width], 'orb', down))]
  transfers between devices with their start and end apart: 16 -> 17, of which waited for: 7 -> 11; matrix products, arithmetic and copies ran while one was open for 11% -> 16% of each run, Pallas kernels for 9% -> 9%
where the time goes in v3:
time: 527 us; the launch traced here: 521 us
  waiting for transfers between devices  238 us (45%)
  Pallas kernels  111 us (21%)
  starting transfers between devices  73.3 us (14%)
  local copies, waits for them, and re-layouts  55.1 us (10%)
  matrix products  29.3 us (6%)
  loops' own time  6.16 us (1%)
  other arithmetic  5.55 us (1%)
    all_to_all x1, waiting for transfers between devices, slab_plan(): exchange(leaving(0, capacity))  134 us
    pallas_call x2, Pallas kernels, slab_plan(): pl.pallas_call(functools.partial(force_kernel, n_orb, before, polynomial(...  57.2 us
    ppermute x5, waiting for transfers between devices, reduce_parts(): lax.ppermute(sent, 'orb', [(d, d ^ bit) for d in range(n_orb)])  55.9 us
    dot_general x2, matrix products, against(): lax.dot_general(left, rounded.reshape(n_orb * capacity, -1), (((1,), (1,)...  29.3 us
    all_to_all x1, starting transfers between devices, slab_plan(): returned = exchange(rounded.reshape(n_orb, capacity, planes, rows, LANES))  25.8 us
    ppermute x4, waiting for transfers between devices, halo_of(): sides.append(lax.ppermute(density[:, :width], 'orb', down))  24.2 us
    pallas_call x2, Pallas kernels, leaving(): pl.pallas_call(spread_kernel, grid_spec=pltpu.PrefetchScalarGridSpec(num_...  23.5 us
    dot_general x3, local copies, waits for them, and re-layouts, against(): lax.dot_general(left, rounded.reshape(n_orb * capacity, -1), (((1,), (1,)...  23.5 us
  transfers between devices with their start and end apart: 17, of which 11 were waited for; matrix products, arithmetic and copies ran while one was open for 16% of the time, Pallas kernels for 9%

profile of v3, /device:TPU:0, one launch (start us, length us, event | category | flops | bytes accessed | tf_op | source)
XLA Modules:
  0.0 520.8 jit_solution(10872437752510674292)
XLA Ops:
  1.9 7.3 %all-to-all-start.5 = ((s32[32,4,4]{2,1,0:T(4,128)}), s32[32,4,4]{2,1,0:T(4,128)S(1)}, u32[]{:S(2)}, u32[]{:S(2)}) async-start(s32[32,4,4]{2,1,0:T(4,128)} %broadcast_in_dim.239), calls=%async_computation.5 | async-start | bytes 131072 | tf_op jit(solution)/shard_map/all_to_all | solution.py:362
  9.3 7.2 %all-to-all-done.5 = s32[32,4,4]{2,1,0:T(4,128)S(1)} async-done(((s32[32,4,4]{2,1,0:T(4,128)}), s32[32,4,4]{2,1,0:T(4,128)S(1)}, u32[]{:S(2)}, u32[]{:S(2)}) %all-to-all-start.5) | async-done | bytes 2080 | tf_op jit(solution)/shard_map/all_to_all | solution.py:362
  18.5 501.1 %conditional.1 = (f32[16,64,4096]{2,1,0:T(8,128)}, f32[1,256]{1,0:T(1,128)}, f32[16]{0:T(128)}) conditional(s32[]{:T(128)} %convert_element_type.19, (s32[32,16]{0,1:T(8,128)S(1)}, s32[128,4]{1,0:T(8,128)S(1)}, (), s32[32,16]{0,1:T(8,128)S(1)}, (), /*index=5*/bf16[16,64,4096]{2,1,0:T(8,128)(2,1)}, s32[32,2]{0,1:T(2,128)}, (), s32[]{:T(128)}, ...), branch_computations={%region_5.14_spmd, %region_10.19_spmd} | conditional | flops 4735760384 | bytes 303070304 | solution.py:382
  24.2 16.5 %branch_1_fun.7 = bf16[32,12,2,32,128]{4,3,2,1,0:T(8,128)(2,1)} custom-call(s32[16]{0:T(128)} %select_reduce_fusion.9.chosen, bf16[16,64,4096]{2,1,0:T(8,128)(2,1)} %get-tuple-element.78.own), custom_call_target="tpu_custom_call" | custom-call | tf_op jit(solution)/shard_map/cond/branch_1_fun/pallas_call | solution.py:395
  40.6 3.6 all-to-all-start.2
  50.0 133.5 %all-to-all-done.2 = bf16[32,12,2,32,128]{4,3,2,1,0:T(8,128)(2,1)} async-done(((bf16[32,12,2,32,128]{4,3,2,1,0:T(8,128)(2,1)}), bf16[32,12,2,32,128]{4,3,2,1,0:T(8,128)(2,1)}, u32[]{:S(2)}, u32[]{:S(2)}) %all-to-all-start.2) | async-done | bytes 6291488 | tf_op jit(solution)/shard_map/cond/branch_1_fun/all_to_all | solution.py:411
  183.6 5.7 %branch_1_fun.9 = bf16[64,2,32,128]{3,2,1,0:T(8,128)(2,1)} custom-call(s32[64,4]{1,0:T(8,128)} %get-tuple-element.227.refs.rest_4_, bf16[384,2,32,128]{3,2,1,0:T(8,128)(2,1)} %bitcast.39.slab), custom_call_target="tpu_custom_call" | custom-call | flops 25600000 | bytes 12000000 | tf_op jit(solution)/shard_map/cond/branch_1_fun/pallas_call | solution.py:431
  193.4 6.2 %collective-permute-start.15 = (bf16[64,1,32,128]{3,2,1,0:T(8,128)(2,1)S(1)}, bf16[64,1,32,128]{3,2,1,0:T(8,128)(2,1)}, u32[]{:S(2)}, u32[]{:S(2)}) collective-permute-start(bf16[64,1,32,128]{3,2,1,0:T(8,128)(2,1)S(1)} %get-tuple-element.224), channel_id=1, source_target_pairs={{0,2},{1,3},{2,6},{3,7},{6,4},{7,5},{4,12},{5,13},{12,14},{13,15},... | collective-permute-start | bytes 1572872 | tf_op jit(solution)/shard_map/cond/branch_1_fun/ppermute | solution.py:451
  201.5 7.1 %branch_1_fun.13 = bf16[32,4,2,32,128]{4,3,2,1,0:T(8,128)(2,1)} custom-call(s32[16]{0:T(128)} %select_reduce_fusion.9.chosen, bf16[16,64,4096]{2,1,0:T(8,128)(2,1)} %get-tuple-element.78.own), custom_call_target="tpu_custom_call" | custom-call | tf_op jit(solution)/shard_map/cond/branch_1_fun/pallas_call | solution.py:395
  211.1 8.8 %collective-permute-done.16.rest_3_ = bf16[64,1,32,128]{3,2,1,0:T(8,128)(2,1)} collective-permute-done((bf16[64,1,32,128]{3,2,1,0:T(8,128)(2,1)S(1)}, bf16[64,1,32,128]{3,2,1,0:T(8,128)(2,1)}, u32[]{:S(2)}, u32[]{:S(2)}) %collective-permute-start.16) | collective-permute-done | bytes 524320 | tf_op jit(solution)/shard_map/cond/branch_1_fun/ppermute | solution.py:453
  221.9 24.7 %branch_1_fun.10.rest_5_ = f32[64,2,2,32,128]{4,3,2,1,0:T(8,128)} custom-call(s32[64,4]{1,0:T(8,128)} %get-tuple-element.227.refs.rest_4_, s32[1]{0:T(128)S(6)} %select_n.365.place, bf16[384,2,32,128]{3,2,1,0:T(8,128)(2,1)} %bitcast.39.slab, bf16[64,2,32,128]{3,2,1,0:T(8,128)(2,1)} %copy-done.7, bf16[64,2,32,128]{3,2,1,0:T(8,128)(2,1)} %copy-done.8, ...), custom_call_target="tpu_custom_call" | custom-call | flops 128000000 | bytes 20000000 | tf_op jit(solution)/shard_map/cond/branch_1_fun/pallas_call | solution.py:467
  246.6 6.1 %all-to-all-start.4 = ((bf16[32,4,2,32,128]{4,3,2,1,0:T(8,128)(2,1)}), bf16[32,4,2,32,128]{4,3,2,1,0:T(8,128)(2,1)S(1)}, u32[]{:S(2)}, u32[]{:S(2)}) async-start(bf16[32,4,2,32,128]{4,3,2,1,0:T(8,128)(2,1)} %branch_1_fun.13), calls=%async_computation.4 | async-start | bytes 4194304 | tf_op jit(solution)/shard_map/cond/branch_1_fun/all_to_all | solution.py:483
  252.7 5.8 %branch_1_fun.8 = bf16[64,2,32,128]{3,2,1,0:T(8,128)(2,1)} custom-call(s32[64,4]{1,0:T(8,128)} %get-tuple-element.228.refs, bf16[384,2,32,128]{3,2,1,0:T(8,128)(2,1)} %bitcast.39.slab), custom_call_target="tpu_custom_call" | custom-call | flops 25600000 | bytes 12000000 | tf_op jit(solution)/shard_map/cond/branch_1_fun/pallas_call | solution.py:431
  259.8 3.1 collective-permute-start.9
  264.2 3.6 collective-permute-start.11
  269.1 15.4 %collective-permute-done.11.rest_2_ = bf16[64,1,32,128]{3,2,1,0:T(8,128)(2,1)S(1)} collective-permute-done((bf16[64,1,32,128]{3,2,1,0:T(8,128)(2,1)S(1)}, bf16[64,1,32,128]{3,2,1,0:T(8,128)(2,1)S(1)}, u32[]{:S(2)}, u32[]{:S(2)}) %collective-permute-start.11) | collective-permute-done | bytes 524320 | tf_op jit(solution)/shard_map/cond/branch_1_fun/ppermute | solution.py:451
  284.5 15.3 %collective-permute-done.12.rest_3_ = bf16[64,1,32,128]{3,2,1,0:T(8,128)(2,1)S(1)} collective-permute-done((bf16[64,1,32,128]{3,2,1,0:T(8,128)(2,1)S(1)}, bf16[64,1,32,128]{3,2,1,0:T(8,128)(2,1)S(1)}, u32[]{:S(2)}, u32[]{:S(2)}) %collective-permute-start.12) | collective-permute-done | bytes 524320 | tf_op jit(solution)/shard_map/cond/branch_1_fun/ppermute | solution.py:453
  302.0 32.5 %branch_1_fun.11 = bf16[384,2,32,128]{3,2,1,0:T(8,128)(2,1)} custom-call(s32[64,4]{1,0:T(8,128)} %get-tuple-element.228.refs, s32[1]{0:T(128)S(6)} %select_n.365.place, bf16[384,2,32,128]{3,2,1,0:T(8,128)(2,1)} %bitcast.39.slab, bf16[64,2,32,128]{3,2,1,0:T(8,128)(2,1)} %copy-done.6, bf16[64,2,32,128]{3,2,1,0:T(8,128)(2,1)} %copy-done.5, ...), custom_call_target="tpu_custom_call" | custom-call | flops 192000000 | bytes 30000000 | tf_op jit(solution)/shard_map/cond/branch_1_fun/pallas_call | solution.py:489
  334.5 25.8 %all-to-all-start.3 = ((bf16[32,12,2,32,128]{4,3,2,1,0:T(8,128)(2,1)}), bf16[32,12,2,32,128]{4,3,2,1,0:T(8,128)(2,1)}, u32[]{:S(2)}, u32[]{:S(2)}) async-start(bf16[32,12,2,32,128]{4,3,2,1,0:T(8,128)(2,1)} %bitcast.255), calls=%async_computation.3 | async-start | bytes 12582912 | tf_op jit(solution)/shard_map/cond/branch_1_fun/all_to_all | solution.py:501
  363.2 7.6 %copy.242 = bf16[32,12,2,32,128]{4,3,2,0,1:T(8,128)(2,1)} copy(bf16[32,12,2,32,128]{4,3,2,1,0:T(8,128)(2,1)} %all-to-all-done.2) | data formatting | bytes 12582912 | tf_op jit(solution)/shard_map/cond/branch_1_fun/all_to_all | solution.py:411
  370.9 10.3 %reshape.663 = bf16[32,12,8192,1]{2,0,1,3:T(8,128)(2,1)} reshape(bf16[32,12,2,32,128]{4,3,2,0,1:T(8,128)(2,1)} %copy.242) | data formatting | bytes 12582912 | tf_op jit(solution)/shard_map/cond/branch_1_fun/dot_general | solution.py:524
  381.2 11.1 %dot_general.10 = bf16[32,12,8192]{2,1,0:T(8,128)(2,1)} reshape(bf16[384,2,32,128]{3,2,1,0:T(8,128)(2,1)} %branch_1_fun.11) | data formatting | bytes 12582912 | tf_op jit(solution)/shard_map/cond/branch_1_fun/dot_general | solution.py:524
  392.3 16.9 %select_reduce_fusion.5 = (f32[32,12]{0,1:T(8,128)S(1)}, f32[32,12,32,12]{0,2,3,1:T(8,128)}) fusion(pred[12,12]{1,0:T(8,128)(4,1)S(1)} %iota_compare_fusion.11, pred[32,32]{0,1:T(8,128)(4,1)S(1)} %iota_compare_fusion.10, bf16[32,12,8192]{2,1,0:T(8,128)(2,1)} %dot_general.10, bf16[32,12,8192,1]{2,0,1,3:T(8,128)(2,1)} %reshape.663), kind=kOutput, calls=%fused_computation.99 | convolution fusion | flops 2416360960 | bytes 13175440 | tf_op jit(solution)/shard_map/cond/branch_1_fun/dot_general | solution.py:524
  412.1 12.4 %fusion.18 = f32[32,4,32,12]{0,2,3,1:T(8,128)S(1)} fusion(bf16[32,12,8192]{2,1,0:T(8,128)(2,1)} %dot_general.10, bf16[32,4,8192,1]{2,1,0,3:T(4,128)(2,1)} %bitcast.260), kind=kOutput, calls=%fused_computation.91 | convolution fusion | flops 805306368 | bytes 8585216 | tf_op jit(solution)/shard_map/cond/branch_1_fun/dot_general | solution.py:524
  425.1 2.4 copy.247
  427.4 2.9 reshape.403
  435.1 2.6 collective-permute-done.18
  439.4 3.2 collective-permute-done.19
  444.2 22.6 %collective-permute-done.20 = f32[2,8,128]{2,1,0:T(8,128)S(1)} collective-permute-done((f32[2,8,128]{2,1,0:T(8,128)S(1)}, f32[2,8,128]{2,1,0:T(8,128)S(1)}, u32[]{:S(2)}, u32[]{:S(2)}) %collective-permute-start.20) | collective-permute-done | bytes 8224 | tf_op jit(solution)/shard_map/cond/branch_1_fun/ppermute | solution.py:346
  466.9 5.8 %collective-permute-start.21 = (f32[1,8,128]{2,1,0:T(8,128)S(1)}, f32[1,8,128]{2,1,0:T(8,128)S(1)}, u32[]{:S(2)}, u32[]{:S(2)}) collective-permute-start(f32[1,8,128]{2,1,0:T(8,128)S(1)} %select_bitcast_fusion.9), channel_id=1, source_target_pairs={{0,16},{1,17},{2,18},{3,19},{4,20},{5,21},{6,22},{7,23},{8,24},{9,... | collective-permute-start | bytes 12296 | tf_op jit(solution)/shard_map/cond/branch_1_fun/ppermute | solution.py:346
  473.2 26.3 %collective-permute-done.21 = f32[1,8,128]{2,1,0:T(8,128)S(1)} collective-permute-done((f32[1,8,128]{2,1,0:T(8,128)S(1)}, f32[1,8,128]{2,1,0:T(8,128)S(1)}, u32[]{:S(2)}, u32[]{:S(2)}) %collective-permute-start.21) | collective-permute-done | bytes 4128 | tf_op jit(solution)/shard_map/cond/branch_1_fun/ppermute | solution.py:346
  500.6 18.8 %branch_1_fun.12 = f32[16,64,4096]{2,1,0:T(8,128)} custom-call(s32[32]{0:T(128)} %pad_add_fusion.3.slots, bf16[32,12,2,32,128]{4,3,2,1,0:T(8,128)(2,1)} %all-to-all-done.3.back), custom_call_target="tpu_custom_call" | custom-call | flops 4000000 | bytes 60000000 | tf_op jit(solution)/shard_map/cond/branch_1_fun/pallas_call | solution.py:504
  (114 shorter events, 41.1 us)
Async XLA Ops:
  1.9 14.5 %all-to-all-start.5 = ((s32[32,4,4]{2,1,0:T(4,128)}), s32[32,4,4]{2,1,0:T(4,128)S(1)}, u32[]{:S(2)}, u32[]{:S(2)}) async-start(s32[32,4,4]{2,1,0:T(4,128)} %broadcast_in_dim.239), calls=%async_computation.5 | async-start | bytes 131072 | tf_op jit(solution)/shard_map/all_to_all | solution.py:362
  40.6 143.0 %all-to-all-start.2 = ((bf16[32,12,2,32,128]{4,3,2,1,0:T(8,128)(2,1)}), bf16[32,12,2,32,128]{4,3,2,1,0:T(8,128)(2,1)}, u32[]{:S(2)}, u32[]{:S(2)}) async-start(bf16[32,12,2,32,128]{4,3,2,1,0:T(8,128)(2,1)} %branch_1_fun.7), calls=%async_computation.2 | async-start | bytes 12582912 | tf_op jit(solution)/shard_map/cond/branch_1_fun/all_to_all | solution.py:411
  46.6 0.7 copy-start
  189.3 30.6 %collective-permute-start.13 = (bf16[64,2,32,128]{3,2,1,0:T(8,128)(2,1)}, bf16[64,2,32,128]{3,2,1,0:T(8,128)(2,1)S(1)}, u32[]{:S(2)}, u32[]{:S(2)}) collective-permute-start(bf16[64,2,32,128]{3,2,1,0:T(8,128)(2,1)} %branch_1_fun.9), channel_id=1, source_target_pairs={{0,1},{1,2},{2,3},{3,6},{6,7},{7,4},{4,5},{5,12},{12,13},{13,14},{... | collective-permute-start | bytes 3145736 | tf_op jit(solution)/shard_map/cond/branch_1_fun/ppermute | solution.py:451
  190.8 29.1 %collective-permute-start.14 = (bf16[64,2,32,128]{3,2,1,0:T(8,128)(2,1)}, bf16[64,2,32,128]{3,2,1,0:T(8,128)(2,1)S(1)}, u32[]{:S(2)}, u32[]{:S(2)}) collective-permute-start(bf16[64,2,32,128]{3,2,1,0:T(8,128)(2,1)} %branch_1_fun.9), channel_id=1, source_target_pairs={{1,0},{2,1},{3,2},{6,3},{7,6},{4,7},{5,4},{12,5},{13,12},{14,13},{... | collective-permute-start | bytes 3145736 | tf_op jit(solution)/shard_map/cond/branch_1_fun/ppermute | solution.py:453
  193.4 17.7 %collective-permute-start.15 = (bf16[64,1,32,128]{3,2,1,0:T(8,128)(2,1)S(1)}, bf16[64,1,32,128]{3,2,1,0:T(8,128)(2,1)}, u32[]{:S(2)}, u32[]{:S(2)}) collective-permute-start(bf16[64,1,32,128]{3,2,1,0:T(8,128)(2,1)S(1)} %get-tuple-element.224), channel_id=1, source_target_pairs={{0,2},{1,3},{2,6},{3,7},{6,4},{7,5},{4,12},{5,13},{12,14},{13,15},... | collective-permute-start | bytes 1572872 | tf_op jit(solution)/shard_map/cond/branch_1_fun/ppermute | solution.py:451
  199.6 20.3 %collective-permute-start.16 = (bf16[64,1,32,128]{3,2,1,0:T(8,128)(2,1)S(1)}, bf16[64,1,32,128]{3,2,1,0:T(8,128)(2,1)}, u32[]{:S(2)}, u32[]{:S(2)}) collective-permute-start(bf16[64,1,32,128]{3,2,1,0:T(8,128)(2,1)S(1)} %get-tuple-element.223), channel_id=1, source_target_pairs={{2,0},{3,1},{6,2},{7,3},{4,6},{5,7},{12,4},{13,5},{14,12},{15,13},... | collective-permute-start | bytes 1572872 | tf_op jit(solution)/shard_map/cond/branch_1_fun/ppermute | solution.py:453
  219.9 1.0 copy-start.7
  220.9 1.0 copy-start.8
  246.6 87.9 %all-to-all-start.4 = ((bf16[32,4,2,32,128]{4,3,2,1,0:T(8,128)(2,1)}), bf16[32,4,2,32,128]{4,3,2,1,0:T(8,128)(2,1)S(1)}, u32[]{:S(2)}, u32[]{:S(2)}) async-start(bf16[32,4,2,32,128]{4,3,2,1,0:T(8,128)(2,1)} %branch_1_fun.13), calls=%async_computation.4 | async-start | bytes 4194304 | tf_op jit(solution)/shard_map/cond/branch_1_fun/all_to_all | solution.py:483
  258.5 41.4 %collective-permute-start.10 = (bf16[64,2,32,128]{3,2,1,0:T(8,128)(2,1)}, bf16[64,2,32,128]{3,2,1,0:T(8,128)(2,1)S(1)}, u32[]{:S(2)}, u32[]{:S(2)}) collective-permute-start(bf16[64,2,32,128]{3,2,1,0:T(8,128)(2,1)} %branch_1_fun.8), channel_id=1, source_target_pairs={{1,0},{2,1},{3,2},{6,3},{7,6},{4,7},{5,4},{12,5},{13,12},{14,13},{... | collective-permute-start | bytes 3145736 | tf_op jit(solution)/shard_map/cond/branch_1_fun/ppermute | solution.py:453
  259.8 40.1 %collective-permute-start.9 = (bf16[64,2,32,128]{3,2,1,0:T(8,128)(2,1)}, bf16[64,2,32,128]{3,2,1,0:T(8,128)(2,1)S(1)}, u32[]{:S(2)}, u32[]{:S(2)}) collective-permute-start(bf16[64,2,32,128]{3,2,1,0:T(8,128)(2,1)} %branch_1_fun.8), channel_id=1, source_target_pairs={{0,1},{1,2},{2,3},{3,6},{6,7},{7,4},{4,5},{5,12},{12,13},{13,14},{... | collective-permute-start | bytes 3145736 | tf_op jit(solution)/shard_map/cond/branch_1_fun/ppermute | solution.py:451
  264.2 20.3 %collective-permute-start.11 = (bf16[64,1,32,128]{3,2,1,0:T(8,128)(2,1)S(1)}, bf16[64,1,32,128]{3,2,1,0:T(8,128)(2,1)S(1)}, u32[]{:S(2)}, u32[]{:S(2)}) collective-permute-start(bf16[64,1,32,128]{3,2,1,0:T(8,128)(2,1)S(1)} %get-tuple-element.226), channel_id=1, source_target_pairs={{0,2},{1,3},{2,6},{3,7},{6,4},{7,5},{4,12},{5,13},{12,14},{13,15},... | collective-permute-start | bytes 1572872 | tf_op jit(solution)/shard_map/cond/branch_1_fun/ppermute | solution.py:451
  267.8 32.0 %collective-permute-start.12 = (bf16[64,1,32,128]{3,2,1,0:T(8,128)(2,1)S(1)}, bf16[64,1,32,128]{3,2,1,0:T(8,128)(2,1)S(1)}, u32[]{:S(2)}, u32[]{:S(2)}) collective-permute-start(bf16[64,1,32,128]{3,2,1,0:T(8,128)(2,1)S(1)} %get-tuple-element.225), channel_id=1, source_target_pairs={{2,0},{3,1},{6,2},{7,3},{4,6},{5,7},{12,4},{13,5},{14,12},{15,13},... | collective-permute-start | bytes 1572872 | tf_op jit(solution)/shard_map/cond/branch_1_fun/ppermute | solution.py:453
  284.5 15.4 %copy-start.9 = (bf16[64,1,32,128]{3,2,1,0:T(8,128)(2,1)}, bf16[64,1,32,128]{3,2,1,0:T(8,128)(2,1)S(1)}, u32[]{:S(2)}) copy-start(bf16[64,1,32,128]{3,2,1,0:T(8,128)(2,1)S(1)} %collective-permute-done.11.rest_2_) | copy-start | bytes 1572868 | tf_op jit(solution)/shard_map/cond
  299.8 0.8 copy-start.10
  299.9 1.2 copy-start.5
  301.0 1.0 copy-start.6
  334.5 25.8 %copy-start.12 = (s32[32,2]{0,1:T(2,128)S(1)}, s32[32,2]{0,1:T(2,128)}, u32[]{:S(2)}) copy-start(s32[32,2]{0,1:T(2,128)} %get-tuple-element.80) | copy-start | bytes 772 | tf_op jit(solution)/shard_map/cond
  334.5 166.1 %all-to-all-start.3 = ((bf16[32,12,2,32,128]{4,3,2,1,0:T(8,128)(2,1)}), bf16[32,12,2,32,128]{4,3,2,1,0:T(8,128)(2,1)}, u32[]{:S(2)}, u32[]{:S(2)}) async-start(bf16[32,12,2,32,128]{4,3,2,1,0:T(8,128)(2,1)} %bitcast.255), calls=%async_computation.3 | async-start | bytes 12582912 | tf_op jit(solution)/shard_map/cond/branch_1_fun/all_to_all | solution.py:501
  412.1 12.4 %copy-start.2 = (f32[32,12,32,12]{0,2,3,1:T(8,128)S(1)}, f32[32,12,32,12]{0,2,3,1:T(8,128)}, u32[]{:S(2)}) copy-start(f32[32,12,32,12]{0,2,3,1:T(8,128)} %get-tuple-element.236) | copy-start | bytes 1769476 | tf_op jit(solution)/shard_map/cond
  432.1 1.3 collective-permute-start.17
  433.4 4.2 collective-permute-start.18
  437.6 5.0 collective-permute-start.19
  442.6 24.2 %collective-permute-start.20 = (f32[2,8,128]{2,1,0:T(8,128)S(1)}, f32[2,8,128]{2,1,0:T(8,128)S(1)}, u32[]{:S(2)}, u32[]{:S(2)}) collective-permute-start(f32[2,8,128]{2,1,0:T(8,128)S(1)} %select_bitcast_fusion.8), channel_id=1, source_target_pairs={{0,8},{1,9},{2,10},{3,11},{4,12},{5,13},{6,14},{7,15},{8,0},{9,1},... | collective-permute-start | bytes 24584 | tf_op jit(solution)/shard_map/cond/branch_1_fun/ppermute | solution.py:346
  466.9 32.6 %collective-permute-start.21 = (f32[1,8,128]{2,1,0:T(8,128)S(1)}, f32[1,8,128]{2,1,0:T(8,128)S(1)}, u32[]{:S(2)}, u32[]{:S(2)}) collective-permute-start(f32[1,8,128]{2,1,0:T(8,128)S(1)} %select_bitcast_fusion.9), channel_id=1, source_target_pairs={{0,16},{1,17},{2,18},{3,19},{4,20},{5,21},{6,22},{7,23},{8,24},{9,... | collective-permute-start | bytes 12296 | tf_op jit(solution)/shard_map/cond/branch_1_fun/ppermute | solution.py:346

commit v4 on v3

--- a/solution.py
+++ b/solution.py
@@ -458,7 +458,10 @@
 
     place = jnp.take(seat, me).reshape(1)
     chunk_refs = [refs[c * chunk:(c + 1) * chunk] for c in range(chunks)]
-    halos = [halo_of(density_of(part)) for part in chunk_refs]
+    densities = [density_of(part) for part in chunk_refs]
+    halos = [halo_of(density) for density in densities]
+    if chunks > 1:
+        chunk_refs[0] = lax.optimization_barrier((chunk_refs[0], densities[-1]))[0]
 
     field_shape = (n_orb * capacity, planes, rows, LANES)
     given = []
@@ -479,7 +482,7 @@
     rest = None
     if fast:
         later = leaving(capacity, orb_dev - capacity)
-        ready = given or sides
+        ready = given + sides
         rest = exchange(lax.optimization_barrier([later] + ready)[0])
         rest = rest.reshape(n_orb * (orb_dev - capacity), -1)
     if given:

time: 527 us -> 490 us (0.930)
  starting transfers between devices: 73.3 us -> 55.4 us
  waiting for transfers between devices: 238 us -> 221 us
    all_to_all x1, starting transfers between devices: 25.8 us -> 3.93 us  [slab_plan(): returned = exchange(rounded.reshape(n_orb, capacity, planes, rows, LANES))]
    ppermute x4, waiting for transfers between devices: 24.2 us -> 6.25 us  [halo_of(): sides.append(lax.ppermute(density[:, :width], 'orb', down))]
    all_to_all x1, waiting for transfers between devices: 0.01 us -> 16.6 us  [slab_plan(): rest = exchange(lax.optimization_barrier([later] + ready)[0])]
    ppermute x4, waiting for transfers between devices: 17.2 us -> 1.84 us  [halo_of(): sides.append(lax.ppermute(density[:, planes - width:], 'orb', up))]
  transfers between devices with their start and end apart: 17 -> 17, of which waited for: 11 -> 10; matrix products, arithmetic and copies ran while one was open for 16% -> 17% of each run, Pallas kernels for 9% -> 14%
where the time goes in v4:
time: 490 us; the launch traced here: 484 us
  waiting for transfers between devices  221 us (45%)
  Pallas kernels  111 us (23%)
  starting transfers between devices  55.4 us (11%)
  local copies, waits for them, and re-layouts  52.9 us (11%)
  matrix products  29.3 us (6%)
  loops' own time  6.15 us (1%)
  other arithmetic  5.64 us (1%)
    all_to_all x1, waiting for transfers between devices, slab_plan(): exchange(leaving(0, capacity))  134 us
    pallas_call x2, Pallas kernels, slab_plan(): pl.pallas_call(functools.partial(force_kernel, n_orb, before, polynomial(...  57.2 us
    ppermute x5, waiting for transfers between devices, reduce_parts(): lax.ppermute(sent, 'orb', [(d, d ^ bit) for d in range(n_orb)])  56 us
    dot_general x2, matrix products, against(): lax.dot_general(left, rounded.reshape(n_orb * capacity, -1), (((1,), (1,)...  29.3 us
    pallas_call x2, Pallas kernels, leaving(): pl.pallas_call(spread_kernel, grid_spec=pltpu.PrefetchScalarGridSpec(num_...  23.5 us
    dot_general x3, local copies, waits for them, and re-layouts, against(): lax.dot_general(left, rounded.reshape(n_orb * capacity, -1), (((1,), (1,)...  23.5 us
    pallas_call x1, Pallas kernels, slab_plan(): pl.pallas_call(collect_kernel, grid_spec=pltpu.PrefetchScalarGridSpec(num...  18.8 us
    ppermute x4, starting transfers between devices, halo_of(): sides.append(lax.ppermute(density[:, planes - width:], 'orb', up))  17.3 us
  transfers between devices with their start and end apart: 17, of which 10 were waited for; matrix products, arithmetic and copies ran while one was open for 17% of the time, Pallas kernels for 14%

profile of v4, /device:TPU:0, one launch (start us, length us, event | category | flops | bytes accessed | tf_op | source)
XLA Modules:
  0.0 484.3 jit_solution(5026787601922161638)
XLA Ops:
  1.9 7.3 %all-to-all-start.5 = ((s32[32,4,4]{2,1,0:T(4,128)}), s32[32,4,4]{2,1,0:T(4,128)S(1)}, u32[]{:S(2)}, u32[]{:S(2)}) async-start(s32[32,4,4]{2,1,0:T(4,128)} %broadcast_in_dim.239), calls=%async_computation.5 | async-start | bytes 131072 | tf_op jit(solution)/shard_map/all_to_all | solution.py:362
  9.3 7.2 %all-to-all-done.5 = s32[32,4,4]{2,1,0:T(4,128)S(1)} async-done(((s32[32,4,4]{2,1,0:T(4,128)}), s32[32,4,4]{2,1,0:T(4,128)S(1)}, u32[]{:S(2)}, u32[]{:S(2)}) %all-to-all-start.5) | async-done | bytes 2080 | tf_op jit(solution)/shard_map/all_to_all | solution.py:362
  18.5 464.6 %conditional.1 = (f32[16,64,4096]{2,1,0:T(8,128)}, f32[1,256]{1,0:T(1,128)}, f32[16]{0:T(128)}) conditional(s32[]{:T(128)} %convert_element_type.19, (s32[32,16]{0,1:T(8,128)S(1)}, s32[128,4]{1,0:T(8,128)S(1)}, (), s32[32,16]{0,1:T(8,128)S(1)}, (), /*index=5*/bf16[16,64,4096]{2,1,0:T(8,128)(2,1)}, s32[32,2]{0,1:T(2,128)}, (), s32[]{:T(128)}, ...), branch_computations={%region_5.14_spmd, %region_10.19_spmd} | conditional | flops 4735760384 | bytes 296778784 | solution.py:382
  24.1 16.5 %branch_1_fun.7 = bf16[32,12,2,32,128]{4,3,2,1,0:T(8,128)(2,1)} custom-call(s32[16]{0:T(128)} %select_reduce_fusion.9.chosen, bf16[16,64,4096]{2,1,0:T(8,128)(2,1)} %get-tuple-element.79.own), custom_call_target="tpu_custom_call" | custom-call | tf_op jit(solution)/shard_map/cond/branch_1_fun/pallas_call | solution.py:395
  40.6 3.6 all-to-all-start.2
  50.0 133.5 %all-to-all-done.2 = bf16[32,12,2,32,128]{4,3,2,1,0:T(8,128)(2,1)} async-done(((bf16[32,12,2,32,128]{4,3,2,1,0:T(8,128)(2,1)}), bf16[32,12,2,32,128]{4,3,2,1,0:T(8,128)(2,1)}, u32[]{:S(2)}, u32[]{:S(2)}) %all-to-all-start.2) | async-done | bytes 6291488 | tf_op jit(solution)/shard_map/cond/branch_1_fun/all_to_all | solution.py:411
  183.5 5.7 %branch_1_fun.9 = bf16[64,2,32,128]{3,2,1,0:T(8,128)(2,1)} custom-call(s32[64,4]{1,0:T(8,128)} %get-tuple-element.50.refs.rest_4_, bf16[384,2,32,128]{3,2,1,0:T(8,128)(2,1)} %bitcast.39.slab), custom_call_target="tpu_custom_call" | custom-call | flops 25600000 | bytes 12000000 | tf_op jit(solution)/shard_map/cond/branch_1_fun/pallas_call | solution.py:431
  192.1 3.8 collective-permute-start.15
  198.5 5.8 %branch_1_fun.8 = bf16[64,2,32,128]{3,2,1,0:T(8,128)(2,1)} custom-call(s32[64,4]{1,0:T(8,128)} %get-tuple-element.229.refs, bf16[384,2,32,128]{3,2,1,0:T(8,128)(2,1)} %bitcast.39.slab), custom_call_target="tpu_custom_call" | custom-call | flops 25600000 | bytes 12000000 | tf_op jit(solution)/shard_map/cond/branch_1_fun/pallas_call | solution.py:431
  207.4 9.7 %collective-permute-start.9 = (bf16[64,2,32,128]{3,2,1,0:T(8,128)(2,1)}, bf16[64,2,32,128]{3,2,1,0:T(8,128)(2,1)S(1)}, u32[]{:S(2)}, u32[]{:S(2)}) collective-permute-start(bf16[64,2,32,128]{3,2,1,0:T(8,128)(2,1)} %branch_1_fun.8), channel_id=1, source_target_pairs={{0,1},{1,2},{2,3},{3,6},{6,7},{7,4},{4,5},{5,12},{12,13},{13,14},{... | collective-permute-start | bytes 3145736 | tf_op jit(solution)/shard_map/cond/branch_1_fun/ppermute | solution.py:451
  217.1 2.3 fusion.47
  219.4 6.2 %collective-permute-done.16.rest_3_ = bf16[64,1,32,128]{3,2,1,0:T(8,128)(2,1)S(1)} collective-permute-done((bf16[64,1,32,128]{3,2,1,0:T(8,128)(2,1)S(1)}, bf16[64,1,32,128]{3,2,1,0:T(8,128)(2,1)S(1)}, u32[]{:S(2)}, u32[]{:S(2)}) %collective-permute-start.16) | collective-permute-done | bytes 524320 | tf_op jit(solution)/shard_map/cond/branch_1_fun/ppermute | solution.py:453
  225.6 2.2 collective-permute-start.11
  229.7 7.1 %branch_1_fun.13 = bf16[32,4,2,32,128]{4,3,2,1,0:T(8,128)(2,1)} custom-call(s32[16]{0:T(128)} %select_reduce_fusion.9.chosen, bf16[16,64,4096]{2,1,0:T(8,128)(2,1)} %get-tuple-element.79.own), custom_call_target="tpu_custom_call" | custom-call | tf_op jit(solution)/shard_map/cond/branch_1_fun/pallas_call | solution.py:395
  237.5 24.7 %branch_1_fun.10.rest_5_ = f32[64,2,2,32,128]{4,3,2,1,0:T(8,128)} custom-call(s32[64,4]{1,0:T(8,128)} %get-tuple-element.50.refs.rest_4_, s32[1]{0:T(128)S(6)} %select_n.365.place, bf16[384,2,32,128]{3,2,1,0:T(8,128)(2,1)} %bitcast.39.slab, bf16[64,2,32,128]{3,2,1,0:T(8,128)(2,1)} %copy-done.7, bf16[64,2,32,128]{3,2,1,0:T(8,128)(2,1)} %collective-permute-done.14.rest_1_, ...), custom_call_target="tpu_custom_call" | custom-call | flops 128000000 | bytes 20000000 | tf_op jit(solution)/shard_map/cond/branch_1_fun/pallas_call | solution.py:470
  263.3 7.0 %all-to-all-start.4 = ((bf16[32,4,2,32,128]{4,3,2,1,0:T(8,128)(2,1)}), bf16[32,4,2,32,128]{4,3,2,1,0:T(8,128)(2,1)S(1)}, u32[]{:S(2)}, u32[]{:S(2)}) async-start(bf16[32,4,2,32,128]{4,3,2,1,0:T(8,128)(2,1)} %branch_1_fun.13), calls=%async_computation.4 | async-start | bytes 4194304 | tf_op jit(solution)/shard_map/cond/branch_1_fun/all_to_all | solution.py:486
  270.3 32.5 %branch_1_fun.11 = bf16[384,2,32,128]{3,2,1,0:T(8,128)(2,1)} custom-call(s32[64,4]{1,0:T(8,128)} %get-tuple-element.229.refs, s32[1]{0:T(128)S(6)} %select_n.365.place, bf16[384,2,32,128]{3,2,1,0:T(8,128)(2,1)} %bitcast.39.slab, bf16[64,2,32,128]{3,2,1,0:T(8,128)(2,1)} %copy-done.5, bf16[64,2,32,128]{3,2,1,0:T(8,128)(2,1)} %copy-done.4, ...), custom_call_target="tpu_custom_call" | custom-call | flops 192000000 | bytes 30000000 | tf_op jit(solution)/shard_map/cond/branch_1_fun/pallas_call | solution.py:492
  302.8 16.6 %all-to-all-done.4 = bf16[32,4,2,32,128]{4,3,2,1,0:T(8,128)(2,1)S(1)} async-done(((bf16[32,4,2,32,128]{4,3,2,1,0:T(8,128)(2,1)}), bf16[32,4,2,32,128]{4,3,2,1,0:T(8,128)(2,1)S(1)}, u32[]{:S(2)}, u32[]{:S(2)}) %all-to-all-start.4) | async-done | bytes 2097184 | tf_op jit(solution)/shard_map/cond/branch_1_fun/all_to_all | solution.py:486
  319.4 3.9 all-to-all-start.3
  326.2 7.6 %copy.242 = bf16[32,12,2,32,128]{4,3,2,0,1:T(8,128)(2,1)} copy(bf16[32,12,2,32,128]{4,3,2,1,0:T(8,128)(2,1)} %all-to-all-done.2) | data formatting | bytes 12582912 | tf_op jit(solution)/shard_map/cond/branch_1_fun/all_to_all | solution.py:411
  333.9 10.3 %reshape.663 = bf16[32,12,8192,1]{2,0,1,3:T(8,128)(2,1)} reshape(bf16[32,12,2,32,128]{4,3,2,0,1:T(8,128)(2,1)} %copy.242) | data formatting | bytes 12582912 | tf_op jit(solution)/shard_map/cond/branch_1_fun/dot_general | solution.py:527
  344.2 11.1 %dot_general.10 = bf16[32,12,8192]{2,1,0:T(8,128)(2,1)} reshape(bf16[384,2,32,128]{3,2,1,0:T(8,128)(2,1)} %branch_1_fun.11) | data formatting | bytes 12582912 | tf_op jit(solution)/shard_map/cond/branch_1_fun/dot_general | solution.py:527
  355.3 16.9 %select_reduce_fusion.5 = (f32[32,12]{0,1:T(8,128)S(1)}, f32[32,12,32,12]{0,2,3,1:T(8,128)}) fusion(pred[12,12]{1,0:T(8,128)(4,1)S(1)} %iota_compare_fusion.11, pred[32,32]{0,1:T(8,128)(4,1)S(1)} %iota_compare_fusion.10, bf16[32,12,8192]{2,1,0:T(8,128)(2,1)} %dot_general.10, bf16[32,12,8192,1]{2,0,1,3:T(8,128)(2,1)} %reshape.663), kind=kOutput, calls=%fused_computation.99 | convolution fusion | flops 2416360960 | bytes 13175440 | tf_op jit(solution)/shard_map/cond/branch_1_fun/dot_general | solution.py:527
  375.1 12.4 %fusion.18 = f32[32,4,32,12]{0,2,3,1:T(8,128)S(1)} fusion(bf16[32,12,8192]{2,1,0:T(8,128)(2,1)} %dot_general.10, bf16[32,4,8192,1]{2,1,0,3:T(4,128)(2,1)} %bitcast.260), kind=kOutput, calls=%fused_computation.91 | convolution fusion | flops 805306368 | bytes 8585216 | tf_op jit(solution)/shard_map/cond/branch_1_fun/dot_general | solution.py:527
  388.1 2.4 copy.247
  390.4 2.9 reshape.403
  397.9 2.5 collective-permute-done.18
  402.3 3.3 collective-permute-done.19
  406.4 22.8 %collective-permute-done.20 = f32[2,8,128]{2,1,0:T(8,128)S(1)} collective-permute-done((f32[2,8,128]{2,1,0:T(8,128)S(1)}, f32[2,8,128]{2,1,0:T(8,128)S(1)}, u32[]{:S(2)}, u32[]{:S(2)}) %collective-permute-start.20) | collective-permute-done | bytes 8224 | tf_op jit(solution)/shard_map/cond/branch_1_fun/ppermute | solution.py:346
  429.2 7.0 %collective-permute-start.21 = (f32[1,8,128]{2,1,0:T(8,128)S(1)}, f32[1,8,128]{2,1,0:T(8,128)S(1)}, u32[]{:S(2)}, u32[]{:S(2)}) collective-permute-start(f32[1,8,128]{2,1,0:T(8,128)S(1)} %select_bitcast_fusion.9), channel_id=1, source_target_pairs={{0,16},{1,17},{2,18},{3,19},{4,20},{5,21},{6,22},{7,23},{8,24},{9,... | collective-permute-start | bytes 12296 | tf_op jit(solution)/shard_map/cond/branch_1_fun/ppermute | solution.py:346
  436.9 26.1 %collective-permute-done.21 = f32[1,8,128]{2,1,0:T(8,128)S(1)} collective-permute-done((f32[1,8,128]{2,1,0:T(8,128)S(1)}, f32[1,8,128]{2,1,0:T(8,128)S(1)}, u32[]{:S(2)}, u32[]{:S(2)}) %collective-permute-start.21) | collective-permute-done | bytes 4128 | tf_op jit(solution)/shard_map/cond/branch_1_fun/ppermute | solution.py:346
  464.1 18.8 %branch_1_fun.12 = f32[16,64,4096]{2,1,0:T(8,128)} custom-call(s32[32]{0:T(128)} %pad_add_fusion.3.slots, bf16[32,12,2,32,128]{4,3,2,1,0:T(8,128)(2,1)} %all-to-all-done.3.back), custom_call_target="tpu_custom_call" | custom-call | flops 4000000 | bytes 60000000 | tf_op jit(solution)/shard_map/cond/branch_1_fun/pallas_call | solution.py:507
  (110 shorter events, 35.8 us)
Async XLA Ops:
  1.9 14.5 %all-to-all-start.5 = ((s32[32,4,4]{2,1,0:T(4,128)}), s32[32,4,4]{2,1,0:T(4,128)S(1)}, u32[]{:S(2)}, u32[]{:S(2)}) async-start(s32[32,4,4]{2,1,0:T(4,128)} %broadcast_in_dim.239), calls=%async_computation.5 | async-start | bytes 131072 | tf_op jit(solution)/shard_map/all_to_all | solution.py:362
  40.6 143.0 %all-to-all-start.2 = ((bf16[32,12,2,32,128]{4,3,2,1,0:T(8,128)(2,1)}), bf16[32,12,2,32,128]{4,3,2,1,0:T(8,128)(2,1)}, u32[]{:S(2)}, u32[]{:S(2)}) async-start(bf16[32,12,2,32,128]{4,3,2,1,0:T(8,128)(2,1)} %branch_1_fun.7), calls=%async_computation.2 | async-start | bytes 12582912 | tf_op jit(solution)/shard_map/cond/branch_1_fun/all_to_all | solution.py:411
  46.5 0.7 copy-start
  189.3 38.6 %collective-permute-start.13 = (bf16[64,2,32,128]{3,2,1,0:T(8,128)(2,1)}, bf16[64,2,32,128]{3,2,1,0:T(8,128)(2,1)S(1)}, u32[]{:S(2)}, u32[]{:S(2)}) collective-permute-start(bf16[64,2,32,128]{3,2,1,0:T(8,128)(2,1)} %branch_1_fun.9), channel_id=1, source_target_pairs={{0,1},{1,2},{2,3},{3,6},{6,7},{7,4},{4,5},{5,12},{12,13},{13,14},{... | collective-permute-start | bytes 3145736 | tf_op jit(solution)/shard_map/cond/branch_1_fun/ppermute | solution.py:451
  192.1 15.3 %collective-permute-start.15 = (bf16[64,1,32,128]{3,2,1,0:T(8,128)(2,1)S(1)}, bf16[64,1,32,128]{3,2,1,0:T(8,128)(2,1)}, u32[]{:S(2)}, u32[]{:S(2)}) collective-permute-start(bf16[64,1,32,128]{3,2,1,0:T(8,128)(2,1)S(1)} %get-tuple-element.225), channel_id=1, source_target_pairs={{0,2},{1,3},{2,6},{3,7},{6,4},{7,5},{4,12},{5,13},{12,14},{13,15},... | collective-permute-start | bytes 1572872 | tf_op jit(solution)/shard_map/cond/branch_1_fun/ppermute | solution.py:451
  195.9 41.6 %collective-permute-start.14 = (bf16[64,2,32,128]{3,2,1,0:T(8,128)(2,1)}, bf16[64,2,32,128]{3,2,1,0:T(8,128)(2,1)}, u32[]{:S(2)}, u32[]{:S(2)}) collective-permute-start(bf16[64,2,32,128]{3,2,1,0:T(8,128)(2,1)} %branch_1_fun.9), channel_id=1, source_target_pairs={{1,0},{2,1},{3,2},{6,3},{7,6},{4,7},{5,4},{12,5},{13,12},{14,13},{... | collective-permute-start | bytes 3145736 | tf_op jit(solution)/shard_map/cond/branch_1_fun/ppermute | solution.py:453
  197.2 28.4 %collective-permute-start.16 = (bf16[64,1,32,128]{3,2,1,0:T(8,128)(2,1)S(1)}, bf16[64,1,32,128]{3,2,1,0:T(8,128)(2,1)S(1)}, u32[]{:S(2)}, u32[]{:S(2)}) collective-permute-start(bf16[64,1,32,128]{3,2,1,0:T(8,128)(2,1)S(1)} %get-tuple-element.224), channel_id=1, source_target_pairs={{2,0},{3,1},{6,2},{7,3},{4,6},{5,7},{12,4},{13,5},{14,12},{15,13},... | collective-permute-start | bytes 1572872 | tf_op jit(solution)/shard_map/cond/branch_1_fun/ppermute | solution.py:453
  204.2 58.0 %collective-permute-start.10 = (bf16[64,2,32,128]{3,2,1,0:T(8,128)(2,1)}, bf16[64,2,32,128]{3,2,1,0:T(8,128)(2,1)S(1)}, u32[]{:S(2)}, u32[]{:S(2)}) collective-permute-start(bf16[64,2,32,128]{3,2,1,0:T(8,128)(2,1)} %branch_1_fun.8), channel_id=1, source_target_pairs={{1,0},{2,1},{3,2},{6,3},{7,6},{4,7},{5,4},{12,5},{13,12},{14,13},{... | collective-permute-start | bytes 3145736 | tf_op jit(solution)/shard_map/cond/branch_1_fun/ppermute | solution.py:453
  207.4 54.9 %collective-permute-start.9 = (bf16[64,2,32,128]{3,2,1,0:T(8,128)(2,1)}, bf16[64,2,32,128]{3,2,1,0:T(8,128)(2,1)S(1)}, u32[]{:S(2)}, u32[]{:S(2)}) collective-permute-start(bf16[64,2,32,128]{3,2,1,0:T(8,128)(2,1)} %branch_1_fun.8), channel_id=1, source_target_pairs={{0,1},{1,2},{2,3},{3,6},{6,7},{7,4},{4,5},{5,12},{12,13},{13,14},{... | collective-permute-start | bytes 3145736 | tf_op jit(solution)/shard_map/cond/branch_1_fun/ppermute | solution.py:451
  225.6 2.2 copy-start.8
  225.6 36.6 %collective-permute-start.11 = (bf16[64,1,32,128]{3,2,1,0:T(8,128)(2,1)}, bf16[64,1,32,128]{3,2,1,0:T(8,128)(2,1)}, u32[]{:S(2)}, u32[]{:S(2)}) collective-permute-start(bf16[64,1,32,128]{3,2,1,0:T(8,128)(2,1)} %get-tuple-element.227), channel_id=1, source_target_pairs={{0,2},{1,3},{2,6},{3,7},{6,4},{7,5},{4,12},{5,13},{12,14},{13,15},... | collective-permute-start | bytes 1572872 | tf_op jit(solution)/shard_map/cond/branch_1_fun/ppermute | solution.py:451
  227.9 9.0 %copy-start.7 = (bf16[64,2,32,128]{3,2,1,0:T(8,128)(2,1)}, bf16[64,2,32,128]{3,2,1,0:T(8,128)(2,1)S(1)}, u32[]{:S(2)}) copy-start(bf16[64,2,32,128]{3,2,1,0:T(8,128)(2,1)S(1)} %collective-permute-done.13.rest_0_) | copy-start | bytes 3145732 | tf_op jit(solution)/shard_map/cond
  227.9 34.4 %collective-permute-start.12 = (bf16[64,1,32,128]{3,2,1,0:T(8,128)(2,1)}, bf16[64,1,32,128]{3,2,1,0:T(8,128)(2,1)}, u32[]{:S(2)}, u32[]{:S(2)}) collective-permute-start(bf16[64,1,32,128]{3,2,1,0:T(8,128)(2,1)} %get-tuple-element.226), channel_id=1, source_target_pairs={{2,0},{3,1},{6,2},{7,3},{4,6},{5,7},{12,4},{13,5},{14,12},{15,13},... | collective-permute-start | bytes 1572872 | tf_op jit(solution)/shard_map/cond/branch_1_fun/ppermute | solution.py:453
  262.2 8.0 %copy-start.4 = (bf16[64,2,32,128]{3,2,1,0:T(8,128)(2,1)}, bf16[64,2,32,128]{3,2,1,0:T(8,128)(2,1)S(1)}, u32[]{:S(2)}) copy-start(bf16[64,2,32,128]{3,2,1,0:T(8,128)(2,1)S(1)} %collective-permute-done.10.rest_1_) | copy-start | bytes 3145732 | tf_op jit(solution)/shard_map/cond
  262.3 1.0 copy-start.5
  263.3 56.1 %all-to-all-start.4 = ((bf16[32,4,2,32,128]{4,3,2,1,0:T(8,128)(2,1)}), bf16[32,4,2,32,128]{4,3,2,1,0:T(8,128)(2,1)S(1)}, u32[]{:S(2)}, u32[]{:S(2)}) async-start(bf16[32,4,2,32,128]{4,3,2,1,0:T(8,128)(2,1)} %branch_1_fun.13), calls=%async_computation.4 | async-start | bytes 4194304 | tf_op jit(solution)/shard_map/cond/branch_1_fun/all_to_all | solution.py:486
  319.3 3.9 copy-start.10
  319.4 144.7 %all-to-all-start.3 = ((bf16[32,12,2,32,128]{4,3,2,1,0:T(8,128)(2,1)}), bf16[32,12,2,32,128]{4,3,2,1,0:T(8,128)(2,1)}, u32[]{:S(2)}, u32[]{:S(2)}) async-start(bf16[32,12,2,32,128]{4,3,2,1,0:T(8,128)(2,1)} %bitcast.255), calls=%async_computation.3 | async-start | bytes 12582912 | tf_op jit(solution)/shard_map/cond/branch_1_fun/all_to_all | solution.py:504
  375.1 12.4 %copy-start.2 = (f32[32,12,32,12]{0,2,3,1:T(8,128)S(1)}, f32[32,12,32,12]{0,2,3,1:T(8,128)}, u32[]{:S(2)}) copy-start(f32[32,12,32,12]{0,2,3,1:T(8,128)} %get-tuple-element.237) | copy-start | bytes 1769476 | tf_op jit(solution)/shard_map/cond
  395.1 1.3 collective-permute-start.17
  396.5 4.0 collective-permute-start.18
  400.5 5.2 %collective-permute-start.19 = (f32[4,8,128]{2,1,0:T(8,128)S(1)}, f32[4,8,128]{2,1,0:T(8,128)S(1)}, u32[]{:S(2)}, u32[]{:S(2)}) collective-permute-start(f32[4,8,128]{2,1,0:T(8,128)S(1)} %select_bitcast_fusion.7), channel_id=1, source_target_pairs={{0,4},{1,5},{2,6},{3,7},{4,0},{5,1},{6,2},{7,3},{8,12},{9,13},{10,... | collective-permute-start | bytes 49160 | tf_op jit(solution)/shard_map/cond/branch_1_fun/ppermute | solution.py:346
  405.6 23.5 %collective-permute-start.20 = (f32[2,8,128]{2,1,0:T(8,128)S(1)}, f32[2,8,128]{2,1,0:T(8,128)S(1)}, u32[]{:S(2)}, u32[]{:S(2)}) collective-permute-start(f32[2,8,128]{2,1,0:T(8,128)S(1)} %select_bitcast_fusion.8), channel_id=1, source_target_pairs={{0,8},{1,9},{2,10},{3,11},{4,12},{5,13},{6,14},{7,15},{8,0},{9,1},... | collective-permute-start | bytes 24584 | tf_op jit(solution)/shard_map/cond/branch_1_fun/ppermute | solution.py:346
  429.2 33.8 %collective-permute-start.21 = (f32[1,8,128]{2,1,0:T(8,128)S(1)}, f32[1,8,128]{2,1,0:T(8,128)S(1)}, u32[]{:S(2)}, u32[]{:S(2)}) collective-permute-start(f32[1,8,128]{2,1,0:T(8,128)S(1)} %select_bitcast_fusion.9), channel_id=1, source_target_pairs={{0,16},{1,17},{2,18},{3,19},{4,20},{5,21},{6,22},{7,23},{8,24},{9,... | collective-permute-start | bytes 12296 | tf_op jit(solution)/shard_map/cond/branch_1_fun/ppermute | solution.py:346
